TPU v7x, 256 devices: a whole 4x4x8 slice. The times are simulated.
256 devices in a mesh: cfg: 2 (over core), tok: 8 (over z), mlp: 16 (over x, y).
Axes of the slice: x: 4, y: 4, z: 8, core: 2. Of those that a mesh axis runs over, the one named last changes fastest.
Arguments:
- hidden: bfloat16 [2, 1536, 4, 3072], P('cfg', ('tok', 'mlp')), may hold values from -6 to 6
- latents: float32 [1536, 4, 64], P(('tok', 'mlp'), None, 'cfg'), may hold values from -6 to 6
- vec: float32 [2, 4, 3072], P('cfg'), may hold values from -9 to 9
- slot_token: int32 [4, 1536], replicated, may hold values from 0 to 1535, each once within a row
- text_len: int32 [2, 4], P('cfg'), may hold values from 64 to 512, as said below
- step_index: int32 [1], replicated, may hold values from 0 to 27
- guidance: float32 [1], replicated, may hold values from 2 to 5
- w_mod: bfloat16 [3072, 15360], P(None, ('tok', 'mlp')), may hold values from -0.109375 to 0.109375
- w_qkv: bfloat16 [1, 3072, 3, 2048], P(None, 'cfg', None, 'mlp'), may hold values from -0.109375 to 0.109375
- w_mlp_in: bfloat16 [1, 3072, 12288], P(None, 'cfg', 'mlp'), may hold values from -0.109375 to 0.109375
- qk_gain: float32 [1, 2, 128], replicated, may hold values from 1.5 to 2.5
- w_attn_out: bfloat16 [1, 2048, 3072], P(None, 'mlp', 'cfg'), may hold values from -0.125 to 0.125
- w_mlp_out: bfloat16 [1, 12288, 3072], P(None, 'mlp', 'cfg'), may hold values from -0.0546875 to 0.0546875
- w_final: bfloat16 [3072, 64], replicated, may hold values from -0.109375 to 0.109375
Outputs:
- velocity: float32 [1536, 4, 64], P(('tok', 'mlp'), None, 'cfg')
- latents_next: float32 [1536, 4, 64], P(('tok', 'mlp'), None, 'cfg')
- stream_out: bfloat16 [2, 1536, 4, 3072], P('cfg', ('tok', 'mlp'))
Inputs may be any that keep to these rules, and one draw needn't show every extreme that they name: `text_len`: real text tokens of each request; its other text slots are padding; exactly one request has all 512. `slot_token`: row p lists the token held by each slot of request p: text tokens are 0 to 511, image tokens follow row by row on the 32 x 32 grid.
All inputs are finite; a program needn't handle non-finite values.
Results may differ from a plain program's by a relative error of at most 0.018.
Values may be sent and summed in bfloat16 or wider, within the bound.
A program may use at most 128 MiB of HBM per device.

v0:
```python
import math

import jax
import jax.numpy as jnp
from jax import lax
from jax.sharding import PartitionSpec as P

LAYERS = 1
SIDE = 32
TXT = 512
STEPS = 28


EPSILON = 1e-06
ROPE_BASE = 10000.0
TIME_SHIFT = 3.0


def swapped(value, axis, apart):
    return lax.ppermute(value, axis, [(i, i ^ 1 << apart) for i in range(lax.axis_size(axis))])


def layer_norm(values):
    average = jnp.mean(values, axis=-1, keepdims=True)
    centred = values - average
    spread = jnp.mean(centred * centred, axis=-1, keepdims=True)
    return centred * lax.rsqrt(spread + EPSILON)


def rms_norm(values, gains):
    return values * lax.rsqrt(jnp.mean(values * values, axis=-1, keepdims=True) + EPSILON) * gains


def rope_table(tokens, head_size, text_count, side_count):
    pair_count = head_size // 2
    first_pairs = head_size // 16
    axis_pairs = (head_size - head_size // 8) // 4
    pair_index = jnp.arange(pair_count).astype(jnp.float32)
    in_rows = (pair_index >= first_pairs) & (pair_index < first_pairs + axis_pairs)
    in_cols = pair_index >= first_pairs + axis_pairs
    log_base = math.log(ROPE_BASE)
    freq_rows = jnp.where(
        in_rows, jnp.exp(-log_base * (pair_index - first_pairs) / axis_pairs), 0.0
    )
    freq_cols = jnp.where(
        in_cols, jnp.exp(-log_base * (pair_index - first_pairs - axis_pairs) / axis_pairs), 0.0
    )
    is_image = tokens >= text_count
    image_pos = jnp.where(is_image, tokens - text_count, 0)
    row_pos = (image_pos // side_count).astype(jnp.float32)
    col_pos = (image_pos % side_count).astype(jnp.float32)
    angles = row_pos[..., None] * freq_rows + col_pos[..., None] * freq_cols
    return (jnp.cos(angles), jnp.sin(angles))


def apply_rope(values, cosine, sine_table):
    even_part = values[..., 0::2]
    odd_part = values[..., 1::2]
    return jnp.concatenate(
        [even_part * cosine - odd_part * sine_table, even_part * sine_table + odd_part * cosine],
        axis=-1,
    )


def sigma_at(position, steps_total):
    remain = 1.0 - position / steps_total
    return TIME_SHIFT * remain / (1.0 + (TIME_SHIFT - 1.0) * remain)


def on_device(
    hidden,
    latents,
    vec,
    slot_token,
    text_len,
    step_index,
    guidance,
    w_mod,
    w_qkv,
    w_mlp_in,
    qk_gain,
    w_attn_out,
    w_mlp_out,
    w_final,
):
    rows_dev = hidden.shape[1]
    prompts = hidden.shape[2]
    model_width = hidden.shape[3]
    head_size = qk_gain.shape[-1]
    mlp_count = lax.axis_size("mlp")
    tile_rows = rows_dev * mlp_count
    tok_index = lax.axis_index("tok")
    mlp_index = lax.axis_index("mlp")
    half_index = lax.axis_index("cfg")
    first_half = half_index == 0
    stream = hidden[0]
    silu_vec = jax.nn.silu(vec[0]).astype(jnp.bfloat16)
    mod_part = jnp.dot(silu_vec, w_mod, preferred_element_type=jnp.float32)
    modulation = lax.all_gather(mod_part, ("tok", "mlp"), axis=1, tiled=True)
    key_valid = ((slot_token >= TXT) | (slot_token < text_len[0][:, None])).astype(jnp.float32)
    tile_tokens = lax.dynamic_slice_in_dim(slot_token, tok_index * tile_rows, tile_rows, 1).T
    cosine, sine_table = rope_table(tile_tokens, head_size, TXT, SIDE)
    shift_mod = modulation[:, 0:model_width]
    scale_mod = modulation[:, model_width : 2 * model_width]
    gate_mod = modulation[:, 2 * model_width : 3 * model_width]
    normed = (
        layer_norm(stream.astype(jnp.float32)) * (1.0 + scale_mod[None]) + shift_mod[None]
    ).astype(jnp.bfloat16)
    tile_input = lax.all_gather(normed, "mlp", axis=0, tiled=True)
    qkv_weight = w_qkv[0]
    unit_weight = w_mlp_in[0]
    qkv_cols = qkv_weight.shape[1] * qkv_weight.shape[2]
    pieces = (
        lax.all_gather(qkv_weight, "cfg", axis=0, tiled=True),
        lax.all_gather(unit_weight, "cfg", axis=0, tiled=True),
    )
    number = pieces[0].shape[0]
    qkv_piece = pieces[0].reshape(number, qkv_cols)
    qkv_pre = jnp.einsum("tpd,dk->tpk", tile_input, qkv_piece, preferred_element_type=jnp.float32)
    unit_pre = jnp.einsum("tpd,dk->tpk", tile_input, pieces[1], preferred_element_type=jnp.float32)
    heads_dev = qkv_weight.shape[2] // head_size
    projected = qkv_pre.reshape(tile_rows, prompts, 3, heads_dev, head_size)
    queries = apply_rope(
        rms_norm(projected[:, :, 0], qk_gain[0, 0]), cosine[:, :, None], sine_table[:, :, None]
    ).astype(jnp.bfloat16)
    keys_rot = apply_rope(
        rms_norm(projected[:, :, 1], qk_gain[0, 1]), cosine[:, :, None], sine_table[:, :, None]
    ).astype(jnp.bfloat16)
    values = projected[:, :, 2].astype(jnp.bfloat16)
    activation = jax.nn.gelu(unit_pre, approximate=True).astype(jnp.bfloat16)
    keys_piece = lax.all_gather(keys_rot, "tok", axis=0, tiled=True)
    values_piece = lax.all_gather(values, "tok", axis=0, tiled=True)
    scores = jnp.einsum(
        "sphe,tphe->phst", queries, keys_piece, preferred_element_type=jnp.float32
    ) / math.sqrt(head_size)
    softened = jnp.exp(scores) * key_valid[:, None, None, :]
    numerator = jnp.einsum(
        "phst,tphe->sphe",
        softened.astype(jnp.bfloat16),
        values_piece,
        preferred_element_type=jnp.float32,
    )
    numerator, denominator = (numerator, jnp.sum(softened, axis=-1))
    attended = (numerator / jnp.transpose(denominator, (2, 0, 1))[..., None]).astype(jnp.bfloat16)
    attended = attended.reshape(tile_rows, prompts, heads_dev * head_size)
    out_attn = lax.all_gather(w_attn_out[0], "cfg", axis=1, tiled=True)
    out_units = lax.all_gather(w_mlp_out[0], "cfg", axis=1, tiled=True)
    branch_out = lax.psum_scatter(
        (
            jnp.einsum("tpk,kd->tpd", attended, out_attn, preferred_element_type=jnp.float32)
            + jnp.einsum("tpk,kd->tpd", activation, out_units, preferred_element_type=jnp.float32)
        ).astype(jnp.bfloat16),
        "mlp",
        scatter_dimension=0,
        tiled=True,
    ).astype(jnp.float32)
    stream = (stream.astype(jnp.float32) + gate_mod[None] * branch_out).astype(jnp.bfloat16)
    final_lo = 3 * LAYERS * model_width
    final_shift = modulation[:, final_lo : final_lo + model_width]
    final_scale = modulation[:, final_lo + model_width : final_lo + 2 * model_width]
    final_normed = (
        layer_norm(stream.astype(jnp.float32)) * (1.0 + final_scale[None]) + final_shift[None]
    ).astype(jnp.bfloat16)
    own_first = (tok_index * mlp_count + mlp_index) * rows_dev
    own_tokens = lax.dynamic_slice_in_dim(slot_token, own_first, rows_dev, 1).T
    half_velocity = jnp.einsum(
        "rpd,dc->rpc", final_normed, w_final, preferred_element_type=jnp.float32
    )
    half_velocity = jnp.where((own_tokens >= TXT)[:, :, None], half_velocity, 0.0)
    channel_half = latents.shape[2]
    own_part = lax.dynamic_slice_in_dim(half_velocity, half_index * channel_half, channel_half, 2)
    sent_part = lax.dynamic_slice_in_dim(
        half_velocity, (1 - half_index) * channel_half, channel_half, 2
    )
    partner = swapped(sent_part, "cfg", 0)
    cond_part = jnp.where(first_half, own_part, partner)
    uncond_part = jnp.where(first_half, partner, own_part)
    velocity = uncond_part + guidance[0] * (cond_part - uncond_part)
    current = step_index[0].astype(jnp.float32)
    step_size = sigma_at(current + 1.0, STEPS) - sigma_at(current, STEPS)
    return (velocity, latents + step_size * velocity, stream[None])


def solution(mesh):
    return jax.shard_map(
        on_device,
        mesh=mesh,
        in_specs=(
            P("cfg", ("tok", "mlp"), None, None),
            P(("tok", "mlp"), None, "cfg"),
            P("cfg", None, None),
            P(),
            P("cfg", None),
            P(),
            P(),
            P(None, ("tok", "mlp")),
            P(None, "cfg", None, "mlp"),
            P(None, "cfg", "mlp"),
            P(),
            P(None, "mlp", "cfg"),
            P(None, "mlp", "cfg"),
            P(),
        ),
        out_specs=(
            P(("tok", "mlp"), None, "cfg"),
            P(("tok", "mlp"), None, "cfg"),
            P("cfg", ("tok", "mlp"), None, None),
        ),
        check_vma=False,
    )
```

profile of v0, /device:TPU:1, one launch (start us, length us, event | category | flops | bytes accessed | tf_op | source)
XLA Modules:
  0.0 687.4 jit_solution(511680488462771938)
XLA Ops:
  7.2 0.0 copy-start
  7.2 0.0 copy-start.10
  7.2 0.0 all-gather.17.cloned.1.call-start
  7.2 2.5 copy.32
  9.8 0.0 all-gather.17.cloned.1.call-update
  9.8 0.0 all-gather.13.cloned.1.call-start
  9.9 0.3 convolution_bitcast_fusion
  10.2 295.8 %all-gather.5 = f32[128,120,4]{1,2,0:T(4,128)S(1)} all-gather(f32[1,120,4]{1,2,0:T(4,128)S(1)} %convolution_bitcast_fusion), channel_id=1, replica_groups=mesh['cfg'=2,'tok'=8,'mlp'=16] {'tok','mlp'}, dimensions={0}, use_global_device_ids=true | all-gather | bytes 247680 | tf_op jit(solution)/shard_map/all_gather | solution.py:99
  305.9 0.3 reshape.291
  306.3 0.2 convert_reduce_fusion.1
  306.5 0.3 fusion.64
  306.8 1.0 fusion.67
  307.9 0.0 all-gather.13.cloned.1.call-update
  307.9 0.0 copy-start.7
  307.9 0.0 all-gather.21.cloned.1.call-start
  307.9 0.7 all-gather.21.cloned.1.call-update
  308.6 0.0 all-gather.23.cloned.1.call-start
  308.7 0.5 all-gather.23.cloned.1.call-update
  309.2 0.0 all-gather.15.cloned.1.call-start
  309.3 0.5 compare_select_fusion
  309.8 0.8 fusion.84
  310.6 0.0 all-gather.17.cloned.1.call-done
  310.6 103.2 %all-gather.13.cloned.1.call-done = bf16[192,4,3072]{2,1,0:T(4,128)(2,1)} async-done(((bf16[12,4,3072]{2,1,0:T(4,128)(2,1)}), bf16[192,4,3072]{2,1,0:T(4,128)(2,1)}) %all-gather.13.cloned.1.call-update) | async-done | bytes 4718608 | tf_op jit(solution)/shard_map/all_gather | solution.py:109
  413.8 5.2 fusion.24
  419.1 0.4 multiply_reduce_fusion.1
  419.4 0.3 multiply_multiply_fusion.2
  419.7 6.6 slice.49
  426.4 7.3 %slice.50 = f32[192,4,1,64]{3,0,1,2:T(8,128)} slice(f32[192,4,1,128]{3,0,1,2:T(8,128)S(1)} %get-tuple-element.18), slice={[0:192:1], [0:4:1], [0:1:1], [1:128:2]} | slice | bytes 393216 | tf_op jit(solution)/shard_map/slice | solution.py:58
  433.7 6.6 slice.53
  440.3 7.5 %slice.54 = f32[192,4,1,64]{3,0,1,2:T(8,128)} slice(f32[192,4,1,128]{3,0,1,2:T(8,128)S(1)} %get-tuple-element.19), slice={[0:192:1], [0:4:1], [0:1:1], [1:128:2]} | slice | bytes 393216 | tf_op jit(solution)/shard_map/slice | solution.py:58
  447.9 4.1 fusion.77
  451.9 0.8 pad_maximum_fusion
  452.7 0.0 all-gather.15.cloned.1.call-update
  452.7 0.0 all-gather.19.cloned.1.call-start
  452.8 0.7 slice.80
  453.5 0.0 all-gather.19.cloned.1.call-update
  453.5 0.0 all-reduce.3.cloned.1.call-start
  453.6 3.4 all-gather.2
  457.0 0.1 or_convert_fusion
  457.1 0.0 all-gather.21.cloned.1.call-done
  457.1 10.6 %fusion.14 = bf16[192,4,768]{2,0,1:T(8,128)(2,1)} fusion(bf16[1,3072,768]{2,1,0:T(8,128)(2,1)} %all-gather.21.cloned.1.call-done, bf16[192,4,3072]{2,1,0:T(4,128)(2,1)} %all-gather.13.cloned.1.call-done), kind=kOutput, calls=%fused_computation.17 | convolution fusion | flops 3629187072 | bytes 10616832 | tf_op jit(solution)/shard_map/tpd,dk->tpk/dot_general | solution.py:120
  467.7 10.2 %fusion = f32[192,4,3072]{2,0,1:T(8,128)} fusion(bf16[192,4,768]{2,0,1:T(8,128)(2,1)} %fusion.14, bf16[1,768,3072]{2,1,0:T(8,128)(2,1)} %all-gather.23.cloned.1.call-done), kind=kOutput, calls=%fused_computation.1 | convolution fusion | flops 3623878656 | bytes 15335424 | tf_op jit(solution)/shard_map/tpk,kd->tpd/dot_general | solution.py:151
  477.9 19.1 %all-gather.15.cloned.1.call-done = bf16[1536,4,1,128]{3,0,1,2:T(8,128)(2,1)} async-done(((bf16[192,4,1,128]{3,0,1,2:T(8,128)(2,1)}), bf16[1536,4,1,128]{3,0,1,2:T(8,128)(2,1)}) %all-gather.15.cloned.1.call-update) | async-done | bytes 1572880 | tf_op jit(solution)/shard_map/all_gather | solution.py:131
  497.0 4.0 fusion.92
  501.1 36.8 %all-gather.19.cloned.1.call-done = bf16[1536,4,1,1,128]{4,0,2,1,3:T(8,128)(2,1)} async-done(((bf16[192,4,1,1,128]{4,0,2,1,3:T(8,128)(2,1)}), bf16[1536,4,1,1,128]{4,0,2,1,3:T(8,128)(2,1)}) %all-gather.19.cloned.1.call-update) | async-done | bytes 1572880 | tf_op jit(solution)/shard_map/all_gather | solution.py:132
  537.9 7.8 %add_convert_fusion = bf16[192,4,3072]{2,0,1:T(8,128)(2,1)} fusion(f32[192,4,3072]{2,0,1:T(8,128)} %fusion, bf16[1536,4,1,1,128]{4,0,2,1,3:T(8,128)(2,1)} %all-gather.19.cloned.1.call-done, bf16[4,192,1536]{2,1,0:T(8,128)(2,1)} %get-tuple-element.36, bf16[1,128,3072]{2,1,0:T(8,128)(2,1)S(1)} %all-gather.2, f32[192,4]{0,1:T(4,128)S(1)} %bitcast.167), kind=kOutput, calls=%fused_computation | convolution fusion | flops 910884864 | bytes 18877440 | tf_op jit(solution)/shard_map/tpk,kd->tpd/dot_general | solution.py:150
  545.7 8.1 %copy.36 = bf16[192,4,3072]{2,1,0:T(4,128)(2,1)} copy(bf16[192,4,3072]{2,0,1:T(8,128)(2,1)} %add_convert_fusion) | data formatting | bytes 9437184 | tf_op jit(solution)/shard_map/convert_element_type | solution.py:152
  553.8 0.0 all-reduce.3.cloned.1.call-update
  553.8 0.0 copy-start.6
  553.9 0.6 copy-done.11
  554.5 0.6 dynamic-slice
  555.7 0.1 fusion.88
  555.8 119.0 %all-reduce.3.cloned.1.call-done = bf16[192,4,3072]{2,1,0:T(4,128)(2,1)} async-done(((bf16[192,4,3072]{2,1,0:T(4,128)(2,1)}), bf16[192,4,3072]{2,1,0:T(4,128)(2,1)}) %all-reduce.3.cloned.1.call-update) | async-done | bytes 4718608
  674.8 1.3 convert_reduce_fusion
  676.1 0.0 copy-start.2
  676.1 0.3 fusion.60
  676.4 0.3 fusion.63
  676.7 0.3 convolution_select_fusion
  677.0 0.1 constant_dynamic-slice_fusion
  677.1 0.7 collective-permute-start
  679.2 0.0 collective-permute-done
  679.2 0.1 copy_add_fusion
  679.3 0.6 copy.39
  679.9 0.6 copy.40
  (27 shorter events, 0.1 us)
Async XLA Ops:
  7.2 2.7 copy-start
  7.2 2.7 copy-start.10
  7.2 299.1 %copy-start.1 = (bf16[1,12,4,3072]{3,2,1,0:T(4,128)(2,1)S(1)}, bf16[1,12,4,3072]{3,2,1,0:T(4,128)(2,1)}, u32[]{:S(2)}) copy-start(bf16[1,12,4,3072]{3,2,1,0:T(4,128)(2,1)} %param.14) | copy-start | bytes 884740
  7.2 303.4 %all-gather.17.cloned.1.call-start = ((), (), s32[]{:S(2)}) async-start(), calls=%async_computation.2 | async-start | bytes 3538944 | tf_op jit(solution)/shard_map/all_gather | solution.py:114
  9.8 404.0 %all-gather.13.cloned.1.call-start = ((), (), s32[]{:S(2)}) async-start(), calls=%async_computation | async-start | bytes 5013504 | tf_op jit(solution)/shard_map/all_gather | solution.py:109
  307.9 2.7 copy-start.7
  307.9 149.2 %all-gather.21.cloned.1.call-start = ((), (), s32[]{:S(2)}) async-start(), calls=%async_computation.4 | async-start | bytes 7077888 | tf_op jit(solution)/shard_map/all_gather | solution.py:115
  308.6 159.0 %all-gather.23.cloned.1.call-start = ((), (), s32[]{:S(2)}) async-start(), calls=%async_computation.5 | async-start | bytes 7077888 | tf_op jit(solution)/shard_map/all_gather | solution.py:147
  309.2 187.8 %all-gather.15.cloned.1.call-start = ((), (), s32[]{:S(2)}) async-start(), calls=%async_computation.1 | async-start | bytes 1769472 | tf_op jit(solution)/shard_map/all_gather | solution.py:131
  447.9 9.2 %copy-start.8 = (s32[1,4]{1,0:T(1,128)S(1)}, s32[1,4]{1,0:T(1,128)}, u32[]{:S(2)}) copy-start(s32[1,4]{1,0:T(1,128)} %param.18) | copy-start | bytes 52
  451.9 5.1 copy-start.5
  452.7 85.2 %all-gather.19.cloned.1.call-start = ((), (), s32[]{:S(2)}) async-start(), calls=%async_computation.3 | async-start | bytes 1769472 | tf_op jit(solution)/shard_map/all_gather | solution.py:132
  453.5 221.3 %all-reduce.3.cloned.1.call-start = ((), (), s32[]{:S(2)}) async-start(), calls=%async_computation.6 | async-start | bytes 9437184
  467.7 29.4 %copy-start.3 = (bf16[192,4,64]{2,0,1:T(8,128)(2,1)S(1)}, bf16[192,4,64]{2,0,1:T(8,128)(2,1)}, u32[]{:S(2)}) copy-start(bf16[192,4,64]{2,0,1:T(8,128)(2,1)} %get-tuple-element.20) | copy-start | bytes 294916
  467.7 29.4 %copy-start.4 = (bf16[192,4,64]{2,0,1:T(8,128)(2,1)S(1)}, bf16[192,4,64]{2,0,1:T(8,128)(2,1)}, u32[]{:S(2)}) copy-start(bf16[192,4,64]{2,0,1:T(8,128)(2,1)} %get-tuple-element.21) | copy-start | bytes 294916
  553.8 0.7 copy-start.11
  553.8 122.9 %copy-start.9 = (bf16[3072,64]{0,1:T(8,128)(2,1)S(1)}, bf16[3072,64]{0,1:T(8,128)(2,1)}, u32[]{:S(2)}) copy-start(bf16[3072,64]{0,1:T(8,128)(2,1)} %param.27) | copy-start | bytes 1179652
  553.8 125.4 %copy-start.6 = (f32[12,4,32]{2,1,0:T(4,128)S(1)}, f32[12,4,32]{2,1,0:T(4,128)}, u32[]{:S(2)}) copy-start(f32[12,4,32]{2,1,0:T(4,128)} %param.15) | copy-start | bytes 18436
  676.1 4.5 copy-start.2
  677.1 2.1 collective-permute-start
Sparse Core Ops, SparseCore 0:
  9.9 20.8 all-gather.16
  308.0 105.7 all-gather.12
  415.6 20.2 all-gather.20
  437.5 21.6 all-gather.22
  460.8 36.1 all-gather.14
  499.3 38.5 all-gather.18
  554.0 120.7 all-reduce.2
where the time goes:
time: 688 us; the launch traced here: 687 us
  blocking collectives  299 us (43%)
  waiting for transfers between devices  279 us (41%)
  local copies, waits for them, and re-layouts  42.4 us (6%)
  matrix products  38.4 us (6%)
  between operations  16.4 us (2%)
  other arithmetic  10.6 us (2%)
    all_gather x1, blocking collectives, on_device(): modulation = lax.all_gather(mod_part, ('tok', 'mlp'), axis=1, tiled=True)  296 us
    unnamed x8, waiting for transfers between devices  120 us
    all_gather x1, waiting for transfers between devices, on_device(): tile_input = lax.all_gather(normed, 'mlp', axis=0, tiled=True)  103 us
    all_gather x1, waiting for transfers between devices, on_device(): values_piece = lax.all_gather(values, 'tok', axis=0, tiled=True)  36.8 us
    all_gather x1, waiting for transfers between devices, on_device(): keys_piece = lax.all_gather(keys_rot, 'tok', axis=0, tiled=True)  19.1 us
    slice x2, local copies, waits for them, and re-layouts, apply_rope(): odd_part = values[..., 1::2]  14.9 us
  transfers between devices with their start and end apart: 8, of which 4 were waited for; matrix products, arithmetic and copies ran while one was open for 10% of the time, Pallas kernels for 0%

commit v1 on v0

v1 whole, which is shorter than its diff:
```python
import math

import jax
import jax.numpy as jnp
from jax import lax
from jax.experimental import pallas as pl
from jax.experimental.pallas import tpu as pltpu
from jax.sharding import PartitionSpec as P

SIDE = 32
TXT = 512
STEPS = 28
EPSILON = 1e-06
ROPE_BASE = 10000.0
TIME_SHIFT = 3.0

MESH = pl.DeviceIdType.MESH
F32 = jnp.float32
BF16 = jnp.bfloat16

D = 3072
HALF = D // 2
HEAD = 128
UNITS = 768
PROMPTS = 4
RING = 4
TOKS = 8
MLPS = 16
PIECE = 24
CHUNK = RING * PIECE
STAGE = 2 * CHUNK
SLOTS = 192
ROWS_OWN = 2 * PIECE
MOD_COLS = 120
CH_HALF = 32


def sigma_at(position, steps_total):
    remain = 1.0 - position / steps_total
    return TIME_SHIFT * remain / (1.0 + (TIME_SHIFT - 1.0) * remain)


def layer_norm(values):
    average = jnp.mean(values, axis=-1, keepdims=True)
    centred = values - average
    spread = jnp.mean(centred * centred, axis=-1, keepdims=True)
    return centred * lax.rsqrt(spread + EPSILON)


def dot_f32(a, b):
    return jnp.dot(a, b, preferred_element_type=F32)


def dot_t(a, b):
    return lax.dot_general(a, b, (((1,), (1,)), ((), ())), preferred_element_type=F32)


def kernel(
    hid_ref, lat_ref, vec_ref, cos_ref, sin_ref, mask_ref, image_ref, scal_ref, gain_ref,
    wmod_hbm, wqkv_hbm, wmi_hbm, wao_hbm, wmo_hbm, wfin_hbm,
    vel_ref, latn_ref, stream_ref,
    X, N, WMOD, WQKV, WMI, WAO, WMO, WFIN, G, MOD, QF, ST, R, OS, OR, ATT,
    ACT, ACC, PS, RB, RC, PS2, RB2, RC2, VS, VR,
    ag_s, ag_r, rs_s, rs_r, w_l, w_s, w_r, m_s, m_r, z_s, z_r, o_s, o_r, v_s, v_r,
):
    c = lax.axis_index("cfg")
    t = lax.axis_index("tok")
    m = lax.axis_index("mlp")
    x, y = m // RING, m % RING
    uv = ((x, y), (y, x))

    def at_uv(k, u, v):
        return u * RING + v if k == 0 else v * RING + u

    def remote(src, dst, ssem, rsem, **where):
        return pltpu.make_async_remote_copy(
            src_ref=src, dst_ref=dst, send_sem=ssem, recv_sem=rsem,
            device_id=where, device_id_type=MESH,
        )

    barrier = pltpu.get_barrier_semaphore()
    for d in range(1, MLPS):
        pl.semaphore_signal(barrier, inc=1, device_id={"mlp": (m + d) % MLPS}, device_id_type=MESH)
    for d in range(1, TOKS):
        pl.semaphore_signal(barrier, inc=1, device_id={"tok": (t + d) % TOKS}, device_id_type=MESH)
    pl.semaphore_signal(barrier, inc=1, device_id={"cfg": 1 - c}, device_id_type=MESH)

    wmod_copy = pltpu.make_async_copy(wmod_hbm, WMOD, w_l.at[0])
    wmod_copy.start()
    k_rows = pl.ds(pl.multiple_of(c * HALF, HALF), HALF)
    weights = (
        [(wqkv_hbm.at[j], WQKV.at[k_rows, pl.ds(j * HEAD, HEAD)]) for j in range(3)]
        + [(wmi_hbm, WMI.at[k_rows]), (wao_hbm, WAO.at[c]), (wmo_hbm, WMO.at[c])]
    )
    local_w = [pltpu.make_async_copy(s, d, w_l.at[1 + i]) for i, (s, d) in enumerate(weights)]
    remote_w = [remote(s, d, w_s.at[i], w_r.at[i], cfg=1 - c) for i, (s, d) in enumerate(weights)]
    fin_copy = pltpu.make_async_copy(wfin_hbm, WFIN, w_l.at[7])

    normed = layer_norm(hid_ref[...].astype(F32)).astype(BF16)
    X[0, y, x] = normed[:PIECE]
    X[1, x, y] = normed[PIECE:]
    pl.semaphore_wait(barrier, MLPS - 1 + TOKS - 1 + 1)

    lo, hi = pl.ds(0, HALF), pl.ds(HALF, HALF)

    def order_u(u, j):
        return (u, (u + 3) % RING, (u + 1) % RING, (u + 2) % RING)[j]

    def ag(k, i):
        u, v = uv[k]
        sems = (ag_s.at[k, i], ag_r.at[k, i])
        up, um = {"mlp": at_uv(k, (u + 1) % RING, v)}, {"mlp": at_uv(k, (u + 3) % RING, v)}
        vp, vm = {"mlp": at_uv(k, u, (v + 1) % RING)}, {"mlp": at_uv(k, u, (v + 3) % RING)}
        if i < 2:
            block = X.at[k, v, u]
            return remote(block, block, *sems, **(up if i == 0 else um))
        if i < 4:
            block = X.at[k, v, (u + (3 if i == 2 else 1)) % RING, :, lo if i == 2 else hi]
            return remote(block, block, *sems, **(up if i == 2 else um))
        if i < 12:
            j, d = (i - 4) // 2, (i - 4) % 2
            block = X.at[k, v, order_u(u, j)]
            return remote(block, block, *sems, **(vp if d == 0 else vm))
        j, d = (i - 12) // 2, (i - 12) % 2
        block = X.at[k, (v + (3 if d == 0 else 1)) % RING, order_u(u, j), :, lo if d == 0 else hi]
        return remote(block, block, *sems, **(vp if d == 0 else vm))

    def ag_start(ids):
        for i in ids:
            for k in range(2):
                ag(k, i).start()

    def ag_recv(ids):
        for i in ids:
            for k in range(2):
                ag(k, i).wait_recv()

    ag_start((0, 1))
    for copy in local_w[:3]:
        copy.start()
    for copy in remote_w[:3]:
        copy.start()
    for i in range(3, 6):
        local_w[i].start()
        remote_w[i].start()
    fin_copy.start()
    ag_start((4, 5))

    wmod_copy.wait()
    vec = vec_ref[...]
    silu_vec = (vec * (1.0 / (1.0 + jnp.exp(-vec)))).astype(BF16)
    G[t, m, :, 0:MOD_COLS] = dot_t(silu_vec, WMOD[...])
    mod1 = [
        remote(G.at[t, m], G.at[t, m], m_s.at[0], m_r.at[0], tok=(t + d) % TOKS) for d in range(1, TOKS)
    ]
    for copy in mod1:
        copy.start()

    ag_recv((0, 1))
    ag_start((2, 3, 6, 7, 8, 9))

    span1 = remote(G.at[pl.ds(0, TOKS - 1), m], G.at[pl.ds(0, TOKS - 1), m], m_s.at[0], m_r.at[0], tok=(t + 1) % TOKS)
    span1.wait_recv()
    mod2 = [
        remote(G.at[:, m], G.at[:, m], m_s.at[1], m_r.at[1], mlp=(m + d) % MLPS) for d in range(1, MLPS)
    ]
    for copy in mod2:
        copy.start()

    ag_recv((2, 3))
    ag_start((10, 11))

    for copy in local_w[:3]:
        copy.wait()
    for copy in remote_w[:3]:
        copy.wait_recv()
    src_col = lax.broadcasted_iota(jnp.int32, (HEAD, HEAD), 0)
    out_col = lax.broadcasted_iota(jnp.int32, (HEAD, HEAD), 1)
    wanted = jnp.where(out_col < HEAD // 2, 2 * out_col, 2 * out_col - HEAD + 1)
    permute = jnp.where(src_col == wanted, 1.0, 0.0).astype(BF16)

    def permute_step(i, carry):
        rows = pl.ds(pl.multiple_of(i * 512, 512), 512)
        for j in range(2):
            cols = pl.ds(j * HEAD, HEAD)
            WQKV[rows, cols] = dot_f32(WQKV[rows, cols], permute).astype(BF16)
        return carry

    lax.fori_loop(0, D // 512, permute_step, 0)

    span2 = remote(
        G.at[:, pl.ds(0, MLPS - 1)], G.at[:, pl.ds(0, MLPS - 1)], m_s.at[1], m_r.at[1], mlp=(m + 1) % MLPS
    )
    span2.wait_recv()
    lane = lax.broadcasted_iota(jnp.int32, (PROMPTS, 128), 1)

    def mod_step(i, carry):
        base = pl.multiple_of(i * (MLPS * MOD_COLS), 128)
        for j in range(15):
            shift = (8 * j) % MOD_COLS
            first = G[i, j]
            if shift:
                first = pltpu.roll(first, 128 - shift, 1)
            second = pltpu.roll(G[i, j + 1], MOD_COLS - shift, 1)
            both = jnp.where(lane < MOD_COLS - shift, first, second)
            MOD[:, pl.ds(base + j * 128, 128)] = jnp.concatenate([both, both], axis=0)
        return carry

    lax.fori_loop(0, TOKS, mod_step, 0)

    for i in range(3, 4):
        local_w[i].wait()
        remote_w[i].wait_recv()

    offsets = (0, 1, 3, 2)

    def chunk_of(s, k):
        return (uv[k][1] + offsets[s]) % RING

    def modulate(s):
        def step(i, carry):
            cols = pl.ds(pl.multiple_of(i * 256, 256), 256)
            scale = 1.0 + MOD[:, pl.ds(pl.multiple_of(D + i * 256, 256), 256)]
            shift = MOD[:, cols]
            for k in range(2):
                ch = chunk_of(s, k)
                for half in range(2):
                    pieces = [X[k, ch, half * 2 + q, :, cols].astype(F32).reshape(3, 8, 256) for q in range(2)]
                    both = jnp.concatenate(pieces, axis=0) * scale[None] + shift[None]
                    N[k * CHUNK + half * 48 : k * CHUNK + half * 48 + 48, cols] = both.reshape(48, 256).astype(BF16)
            return carry

        lax.fori_loop(0, D // 256, step, 0)

    soft_scale = math.log2(math.e) / math.sqrt(HEAD)

    def qkv(s):
        pre = dot_f32(N[...], WQKV[...])
        for j in range(3):
            QF[j] = pre[:, j * HEAD : (j + 1) * HEAD]
        cha, chb = chunk_of(s, 0), chunk_of(s, 1) + RING
        for p in range(PROMPTS):
            rows = pl.ds(p, 2 * PIECE, stride=PROMPTS)
            cosine = jnp.concatenate([cos_ref[p, cha], cos_ref[p, chb]], axis=0)
            sine = jnp.concatenate([sin_ref[p, cha], sin_ref[p, chb]], axis=0)
            outs = []
            for j in range(2):
                val = QF.at[j][rows, :]
                val = val * lax.rsqrt(jnp.mean(val * val, axis=-1, keepdims=True) + EPSILON) * gain_ref[j : j + 1, :]
                outs.append((val * cosine + pltpu.roll(val, HEAD // 2, 1) * sine).astype(BF16))
            outs.append(QF.at[2][rows, :].astype(BF16))
            for place, val in ((0, outs[1]), (1, outs[2]), (2, outs[0])):
                ST[p, cha, place] = val[:PIECE]
                ST[p, chb, place] = val[PIECE:]

    def job(i):
        p = (t // 2 + i) % PROMPTS
        rel = (t - 2 * p + TOKS) % TOKS
        half = 1 - ((rel + 7) % TOKS) // RING
        return p, 2 * p + half, 2 * p + 1 - half

    kv = pl.ds(0, 2)

    def send_stage(s):
        for ch in (chunk_of(s, 0), chunk_of(s, 1) + RING):
            for i in range(PROMPTS):
                p, z_query, z_other = job(i)
                if i == 0:
                    pltpu.make_async_copy(ST.at[p, ch], R.at[t, ch], z_r.at[t]).start()
                else:
                    remote(ST.at[p, ch], R.at[t, ch], z_s.at[i, 0], z_r.at[t], tok=z_query).start()
                remote(ST.at[p, ch, kv], R.at[t, ch, kv], z_s.at[i, 1], z_r.at[t], tok=z_other).start()

    def units(s):
        def step(i, carry):
            cols = pl.ds(pl.multiple_of(i * 256, 256), 256)
            ACT[s, :, cols] = jax.nn.gelu(dot_f32(N[...], WMI[:, cols]), approximate=True).astype(BF16)
            return carry

        lax.fori_loop(0, UNITS // 256, step, 0)

    def units_out(s):
        def step(i, carry):
            cols = pl.ds(pl.multiple_of(i * 256, 256), 256)
            for h in range(2):
                ACC[s, h, :, cols] = dot_f32(ACT[s], WMO[h, :, cols])
            return carry

        lax.fori_loop(0, HALF // 256, step, 0)

    modulate(0)
    qkv(0)
    send_stage(0)
    ag_recv((4, 5))
    ag_start((12, 13))
    units(0)
    ag_recv((6, 7))
    ag_start((14, 15))
    for i in range(4, 6):
        local_w[i].wait()
        remote_w[i].wait_recv()
    ag_recv((8, 9))
    ag_start((16, 17))
    ag_recv((10, 11))
    ag_start((18, 19))
    for s in (1, 2):
        modulate(s)
        qkv(s)
        send_stage(s)
        units(s)
    ag_recv(range(12, 20))
    modulate(3)
    qkv(3)
    send_stage(3)
    units(3)
    for s in range(4):
        units_out(s)

    sign = 1 - 2 * (t % 2)

    def tile(o):
        return (t + TOKS - sign * o) % TOKS

    pltpu.make_async_copy(ST.at[0], R.at[t], z_r.at[t]).wait()
    for o in range(1, TOKS):
        src = tile(o)
        if o < RING:
            remote(R.at[src], R.at[src], z_s.at[0, 0], z_r.at[src], tok=(t + 1) % TOKS).wait_recv()
        else:
            part = R.at[src, :, kv]
            remote(part, part, z_s.at[0, 0], z_r.at[src], tok=(t + 1) % TOKS).wait_recv()
    own_p = t // 2

    def attend(o):
        keys = R[:, :, 0].reshape(TOKS * SLOTS, HEAD)
        vals = R[:, :, 1].reshape(TOKS * SLOTS, HEAD)
        query = R[tile(o), :, 2].reshape(SLOTS, HEAD)
        soft = jnp.exp2(dot_t(query, keys) * soft_scale) * mask_ref[...]
        total = jnp.sum(soft, axis=-1, keepdims=True)
        return (dot_f32(soft.astype(BF16), vals) / total).astype(BF16)

    for o in range(1, RING):
        OS[o] = attend(o)
        remote(OS.at[o], OR.at[own_p], o_s.at[o], o_r.at[own_p], tok=tile(o)).start()
    OR[own_p] = attend(0)

    for i in range(1, PROMPTS):
        p, z_query, _ = job(i)
        remote(OS.at[0], OR.at[p], o_s.at[0], o_r.at[p], tok=z_query).wait_recv()
    for p in range(PROMPTS):
        ATT[pl.ds(p, SLOTS, stride=PROMPTS), :] = OR[p].astype(F32)

    def out_stage(s):
        rows = [
            ATT[pl.ds(pl.multiple_of((k * RING + chunk_of(s, k)) * CHUNK, CHUNK), CHUNK), :] for k in range(2)
        ]
        att = jnp.concatenate(rows, axis=0).astype(BF16)
        for h in range(2):
            for n in range(HALF // 512):
                cols = slice(n * 512, (n + 1) * 512)
                part = dot_f32(att, WAO[h, :, cols]) + ACC[s, h, :, cols]
                for k in range(2):
                    for u in range(RING):
                        first = k * CHUNK + u * PIECE
                        PS[k, chunk_of(s, k), u, :, h * HALF + n * 512 : h * HALF + (n + 1) * 512] = part[
                            first : first + PIECE
                        ].astype(BF16)

    def back_u(u, j):
        return (u + (2, 1, 3, 0)[j]) % RING

    def rs(k, i):
        u, v = uv[k]
        sems = (rs_s.at[k, i], rs_r.at[k, i])
        up, um = {"mlp": at_uv(k, (u + 1) % RING, v)}, {"mlp": at_uv(k, (u + 3) % RING, v)}
        vp, vm = {"mlp": at_uv(k, u, (v + 1) % RING)}, {"mlp": at_uv(k, u, (v + 3) % RING)}
        if i < 16:
            j, d = (i % 8) // 2, i % 2
            where = vp if d == 0 else vm
            if i < 8:
                block = PS.at[k, (v + 2) % RING, back_u(u, j), :, lo if d == 0 else hi]
                return remote(block, RB.at[k, d, j], *sems, **where)
            block = PS.at[k, (v + (1 if d == 0 else 3)) % RING, back_u(u, j)]
            return remote(block, RC.at[k, d, j], *sems, **where)
        d = i % 2
        where = up if d == 0 else um
        if i < 18:
            return remote(PS2.at[k, 0, :, lo if d == 0 else hi], RB2.at[k, d], *sems, **where)
        return remote(PS2.at[k, 1 + d], RC2.at[k, d], *sems, **where)

    out_stage(3)
    for i in range(8):
        for k in range(2):
            rs(k, i).start()
    out_stage(1)
    out_stage(2)
    for j in range(RING):
        for d in range(2):
            for k in range(2):
                u, v = uv[k]
                rs(k, 2 * j + d).wait_recv()
                cols = slice(0, HALF) if d == 0 else slice(HALF, D)
                ch = (v + (1 if d == 0 else 3)) % RING
                PS[k, ch, back_u(u, j), :, cols] = (
                    PS[k, ch, back_u(u, j), :, cols].astype(F32) + RB[k, d, j].astype(F32)
                ).astype(BF16)
                rs(k, 8 + 2 * j + d).start()
    out_stage(0)

    def own_sum(k, j):
        u, v = uv[k]
        for d in range(2):
            rs(k, 8 + 2 * j + d).wait_recv()
        return PS[k, v, back_u(u, j)].astype(F32) + RC[k, 0, j].astype(F32) + RC[k, 1, j].astype(F32)

    for k in range(2):
        PS2[k, 0] = own_sum(k, 0).astype(BF16)
        rs(k, 16).start()
        rs(k, 17).start()
    for d in range(2):
        for k in range(2):
            total = own_sum(k, 1 + d)
            rs(k, 16 + d).wait_recv()
            cols = slice(0, HALF) if d == 0 else slice(HALF, D)
            PS2[k, 1 + d] = total.astype(BF16)
            PS2[k, 1 + d, :, cols] = (total[:, cols] + RB2[k, d].astype(F32)).astype(BF16)
            rs(k, 18 + d).start()
    fin_copy.wait()
    finals = []
    for k in range(2):
        branch = own_sum(k, 3)
        for d in range(2):
            rs(k, 18 + d).wait_recv()
        branch = branch + RC2[k, 0].astype(F32) + RC2[k, 1].astype(F32)
        rows = slice(k * PIECE, (k + 1) * PIECE)
        gated = branch.reshape(3, 8, D) * MOD[:, 2 * D : 3 * D][None]
        stream = (hid_ref[rows, :].astype(F32) + gated.reshape(PIECE, D)).astype(BF16)
        stream_ref[rows, :] = stream
        shaped = layer_norm(stream.astype(F32)).reshape(3, 8, D)
        shaped = shaped * (1.0 + MOD[:, 4 * D : 5 * D])[None] + MOD[:, 3 * D : 4 * D][None]
        finals.append(shaped.reshape(PIECE, D).astype(BF16).astype(F32))
    final_normed = jnp.concatenate(finals, axis=0).astype(BF16)
    half_velocity = dot_t(final_normed, WFIN[...])
    parts = (half_velocity[:, :CH_HALF] * image_ref[...], half_velocity[:, CH_HALF:] * image_ref[...])
    first = c == 0
    VS[...] = jnp.where(first, parts[1], parts[0])
    swap = remote(VS, VR, v_s, v_r, cfg=1 - c)
    swap.start()
    own = jnp.where(first, parts[0], parts[1])
    swap.wait_recv()
    other = VR[...]
    cond = jnp.where(first, own, other)
    uncond = jnp.where(first, other, own)
    velocity = uncond + scal_ref[0:1, :] * (cond - uncond)
    vel_ref[...] = velocity
    latn_ref[...] = lat_ref[...] + scal_ref[1:2, :] * velocity

    swap.wait_send()
    for copy in remote_w:
        copy.wait_send()
    span1.wait_send()
    span2.wait_send()
    for k in range(2):
        for i in range(20):
            ag(k, i).wait_send()
            rs(k, i).wait_send()
    for i in range(PROMPTS):
        p, z_query, z_other = job(i)
        if i:
            remote(ST.at[p], R.at[t], z_s.at[i, 0], z_r.at[t], tok=z_query).wait_send()
        remote(ST.at[p, :, kv], R.at[t, :, kv], z_s.at[i, 1], z_r.at[t], tok=z_other).wait_send()
    for o in range(1, RING):
        remote(OS.at[o], OR.at[own_p], o_s.at[o], o_r.at[own_p], tok=tile(o)).wait_send()


def call_kernel(*operands):
    vmem = pl.BlockSpec(memory_space=pltpu.VMEM)
    hbm = pl.BlockSpec(memory_space=pl.ANY)
    dma = pltpu.SemaphoreType.DMA
    scratch = [
        pltpu.VMEM((2, RING, RING, PIECE, D), BF16),
        pltpu.VMEM((STAGE, D), BF16),
        pltpu.VMEM((MOD_COLS, D), BF16),
        pltpu.VMEM((D, 3 * HEAD), BF16),
        pltpu.VMEM((D, UNITS), BF16),
        pltpu.VMEM((2, HEAD, HALF), BF16),
        pltpu.VMEM((2, UNITS, HALF), BF16),
        pltpu.VMEM((2 * CH_HALF, D), BF16),
        pltpu.VMEM((TOKS, MLPS, PROMPTS, 128), F32),
        pltpu.VMEM((8, 5 * D), F32),
        pltpu.VMEM((3, STAGE, HEAD), F32),
        pltpu.VMEM((PROMPTS, 2 * RING, 3, PIECE, HEAD), BF16),
        pltpu.VMEM((TOKS, 2 * RING, 3, PIECE, HEAD), BF16),
        pltpu.VMEM((RING, SLOTS, HEAD), BF16),
        pltpu.VMEM((PROMPTS, SLOTS, HEAD), BF16),
        pltpu.VMEM((PROMPTS * SLOTS, HEAD), F32),
        pltpu.VMEM((RING, STAGE, UNITS), BF16),
        pltpu.VMEM((RING, 2, STAGE, HALF), F32),
        pltpu.VMEM((2, RING, RING, PIECE, D), BF16),
        pltpu.VMEM((2, 2, RING, PIECE, HALF), BF16),
        pltpu.VMEM((2, 2, RING, PIECE, D), BF16),
        pltpu.VMEM((2, 3, PIECE, D), BF16),
        pltpu.VMEM((2, 2, PIECE, HALF), BF16),
        pltpu.VMEM((2, 2, PIECE, D), BF16),
        pltpu.VMEM((ROWS_OWN, CH_HALF), F32),
        pltpu.VMEM((ROWS_OWN, CH_HALF), F32),
        dma((2, 20)), dma((2, 20)), dma((2, 20)), dma((2, 20)),
        dma((8,)), dma((6,)), dma((6,)), dma((2,)), dma((2,)),
        dma((PROMPTS, 2)), dma((TOKS,)), dma((RING,)), dma((PROMPTS,)), dma, dma,
    ]
    return pl.pallas_call(
        kernel,
        out_shape=(
            jax.ShapeDtypeStruct((ROWS_OWN, CH_HALF), F32),
            jax.ShapeDtypeStruct((ROWS_OWN, CH_HALF), F32),
            jax.ShapeDtypeStruct((ROWS_OWN, D), BF16),
        ),
        in_specs=[vmem] * 9 + [hbm] * 6,
        out_specs=(vmem, vmem, vmem),
        scratch_shapes=scratch,
        compiler_params=pltpu.CompilerParams(
            collective_id=0, has_side_effects=True, vmem_limit_bytes=67043328
        ),
    )(*operands)


def rope_tables(tokens):
    pair_count = HEAD // 2
    first_pairs = HEAD // 16
    axis_pairs = (HEAD - HEAD // 8) // 4
    pair_index = (jnp.arange(HEAD) % pair_count).astype(F32)
    in_rows = (pair_index >= first_pairs) & (pair_index < first_pairs + axis_pairs)
    in_cols = pair_index >= first_pairs + axis_pairs
    log_base = math.log(ROPE_BASE)
    freq_rows = jnp.where(in_rows, jnp.exp(-log_base * (pair_index - first_pairs) / axis_pairs), 0.0)
    freq_cols = jnp.where(in_cols, jnp.exp(-log_base * (pair_index - first_pairs - axis_pairs) / axis_pairs), 0.0)
    is_image = tokens >= TXT
    image_pos = jnp.where(is_image, tokens - TXT, 0)
    row_pos = (image_pos // SIDE).astype(F32)
    col_pos = (image_pos % SIDE).astype(F32)
    angles = row_pos[..., None] * freq_rows + col_pos[..., None] * freq_cols
    side = jnp.where(jnp.arange(HEAD) < pair_count, -1.0, 1.0)
    return jnp.cos(angles), jnp.sin(angles) * side


def on_device(
    hidden, latents, vec, slot_token, text_len, step_index, guidance,
    w_mod, w_qkv, w_mlp_in, qk_gain, w_attn_out, w_mlp_out, w_final,
):
    tok = lax.axis_index("tok")
    mlp = lax.axis_index("mlp")
    rows_dev, prompts = hidden.shape[1], hidden.shape[2]
    split = slot_token.reshape(prompts, TOKS, RING, RING, 2, rows_dev // 2)
    first = split[:, :, :, :, 0].transpose(0, 1, 3, 2, 4).reshape(prompts, TOKS, SLOTS // 2)
    second = split[:, :, :, :, 1].reshape(prompts, TOKS, SLOTS // 2)
    ordered = jnp.concatenate([first, second], axis=2)
    tile_tokens = lax.dynamic_index_in_dim(ordered, tok, 1, keepdims=False)
    cosine, sine = rope_tables(tile_tokens.reshape(prompts, 2 * RING, PIECE))
    own_prompt = tok // 2
    job_tokens = lax.dynamic_index_in_dim(ordered, own_prompt, 0, keepdims=False).reshape(1, TOKS * SLOTS)
    job_len = lax.dynamic_index_in_dim(text_len[0], own_prompt, 0, keepdims=False)
    mask = ((job_tokens >= TXT) | (job_tokens < job_len)).astype(F32)
    own_first = (tok * MLPS + mlp) * rows_dev
    own_tokens = lax.dynamic_slice_in_dim(slot_token, own_first, rows_dev, 1).T.reshape(ROWS_OWN, 1)
    image = jnp.broadcast_to((own_tokens >= TXT).astype(F32), (ROWS_OWN, CH_HALF))
    current = step_index[0].astype(F32)
    step_size = sigma_at(current + 1.0, STEPS) - sigma_at(current, STEPS)
    scalars = jnp.broadcast_to(jnp.stack([guidance[0], step_size])[:, None], (2, CH_HALF))
    gains = qk_gain[0].reshape(2, HEAD // 2, 2).transpose(0, 2, 1).reshape(2, HEAD)
    velocity, latents_next, stream = call_kernel(
        hidden[0].reshape(ROWS_OWN, D), latents.reshape(ROWS_OWN, CH_HALF), vec[0],
        cosine, sine, mask, image, scalars, gains,
        w_mod.T, w_qkv[0].transpose(1, 0, 2), w_mlp_in[0], w_attn_out[0], w_mlp_out[0], w_final.T,
    )
    return (
        velocity.reshape(latents.shape),
        latents_next.reshape(latents.shape),
        stream.reshape(hidden.shape),
    )


def solution(mesh):
    return jax.shard_map(
        on_device,
        mesh=mesh,
        in_specs=(
            P("cfg", ("tok", "mlp"), None, None),
            P(("tok", "mlp"), None, "cfg"),
            P("cfg", None, None),
            P(),
            P("cfg", None),
            P(),
            P(),
            P(None, ("tok", "mlp")),
            P(None, "cfg", None, "mlp"),
            P(None, "cfg", "mlp"),
            P(),
            P(None, "mlp", "cfg"),
            P(None, "mlp", "cfg"),
            P(),
        ),
        out_specs=(
            P(("tok", "mlp"), None, "cfg"),
            P(("tok", "mlp"), None, "cfg"),
            P("cfg", ("tok", "mlp"), None, None),
        ),
        check_vma=False,
    )
```

time: 688 us -> 116 us (0.17)
  blocking collectives: 299 us -> 0 us
  waiting for transfers between devices: 279 us -> 0 us
  Pallas kernels: 0 us -> 94.5 us
  matrix products: 38.4 us -> 0 us
  local copies, waits for them, and re-layouts: 42.4 us -> 14.3 us
  between operations: 16.4 us -> 2.08 us
    all_gather x2 -> x0, blocking collectives: 299 us -> none  [the longest x1 296 us: on_device(): modulation = lax.all_gather(mod_part, ('tok', 'mlp'), axis=1, tiled=True)]
    all_gather x6 -> x0, waiting for transfers between devices: 159 us -> none  [the longest x1 103 us: on_device(): tile_input = lax.all_gather(normed, 'mlp', axis=0, tiled=True)]
    unnamed x8 -> x0, waiting for transfers between devices: 120 us -> none
    pallas_call x0 -> x1, Pallas kernels: none -> 94.5 us  [call_kernel(): pl.pallas_call(kernel, out_shape=(jax.ShapeDtypeStruct((ROWS_OWN, CH_HALF...]
    dot_general x7 -> x0, matrix products: 38.4 us -> none  [the longest x1 10.6 us: on_device(): jnp.einsum('tpd,dk->tpk', tile_input, pieces[1], preferred_element_type=j...]
    slice x5 -> x1, local copies, waits for them, and re-layouts: 28.8 us -> 0.96 us  [on_device(): split[:, :, :, :, 0].transpose(0, 1, 3, 2, 4)]
    convert_element_type x1 -> x3, local copies, waits for them, and re-layouts: 8.11 us -> 0.86 us  [the longest x1 0.68 us: on_device(): mask = ((job_tokens >= TXT) | (job_tokens < job_len)).astype(F32)]
  transfers between devices with their start and end apart: 8 -> 0, of which waited for: 4 -> 0; matrix products, arithmetic and copies ran while one was open for 10% -> 0% of each run, Pallas kernels for 0% -> 0%
where the time goes in v1:
time: 116 us; the launch traced here: 115 us
  Pallas kernels  94.5 us (81%)
  local copies, waits for them, and re-layouts  14.3 us (12%)
  other arithmetic  4.58 us (4%)
  between operations  2.08 us (2%)
    pallas_call x1, Pallas kernels, call_kernel(): pl.pallas_call(kernel, out_shape=(jax.ShapeDtypeStruct((ROWS_OWN, CH_HALF...  94.5 us
    mul x1, other arithmetic, rope_tables(): return (jnp.cos(angles), jnp.sin(angles) * side)  2.87 us
    unnamed x2, local copies, waits for them, and re-layouts  2.69 us

profile of v1, /device:TPU:1, one launch (start us, length us, event | category | flops | bytes accessed | tf_op | source)
XLA Modules:
  0.0 115.5 jit_solution(17567728386025016789)
XLA Ops:
  2.0 0.1 pad_maximum_fusion
  2.1 1.2 %constant_dynamic-slice_fusion = s32[1,1]{1,0:T(1,128)} fusion(s32[1,4]{1,0:T(1,128)} %param.18, s32[]{:T(128)S(6)} %select_n.99), kind=kLoop, calls=%fused_computation.29 | loop fusion | bytes 12 | tf_op jit(solution)/shard_map/jit(dynamic_index_in_dim)/dynamic_slice | solution.py:561
  3.3 0.6 broadcast_in_dim.41.scal_ref
  4.0 0.8 convert_bitcast_fusion
  4.8 0.1 copy.21
  4.9 0.1 reshape.188
  5.0 0.7 broadcast_in_dim.40.image_ref
  5.6 0.8 reshape_squeeze.11
  6.5 0.1 copy.22
  6.5 0.7 reshape.183.gain_ref
  7.2 1.7 %reshape_squeeze.9.hid_ref = bf16[48,3072]{1,0:T(8,128)(2,1)} reshape(bf16[1,12,4,3072]{3,2,1,0:T(4,128)(2,1)} %param.14) | data formatting | bytes 589824 | tf_op jit(solution)/shard_map/reshape;squeeze | solution.py:571
  9.0 1.5 %reshape.181 = s32[4,8,4,4,2,6]{5,4,3,2,1,0:T(2,128)S(1)} reshape(s32[4,1536]{1,0:T(4,128)} %param.17) | data formatting | bytes 49152 | tf_op jit(solution)/shard_map/reshape | solution.py:553
  10.5 1.0 fusion.9
  11.4 0.1 copy.20
  11.5 0.2 reshape.182
  11.8 0.2 reshape_squeeze.10
  12.0 0.1 fusion.6
  12.1 0.7 or_convert_fusion
  12.8 0.7 reshape.187.mask_ref
  13.5 0.1 select_n.91
  13.6 2.9 %sine_multiply_fusion = (f32[4,8,24,128]{3,2,1,0:T(8,128)}, f32[4,8,24,128]{3,2,1,0:T(8,128)}) fusion(f32[128]{0:T(128)S(1)} %compare_select_fusion.1, f32[128]{0:T(128)S(1)} %get-tuple-element.15, f32[4,8,24]{2,1,0:T(8,128)S(1)} %get-tuple-element.14, f32[128]{0:T(128)S(1)} %get-tuple-element.16, f32[4,8,24]{2,1,0:T(8,128)S(1)} %get-tuple-element.13), kind=kLoop, calls=%fused_computation | loop fusion | flops 393216 | bytes 794112 | tf_op jit(solution)/shard_map/mul | solution.py:543
  16.5 94.5 %shard_map.157 = (f32[48,32]{1,0:T(8,128)}, f32[48,32]{1,0:T(8,128)}, bf16[48,3072]{1,0:T(8,128)(2,1)}) custom-call(bf16[48,3072]{1,0:T(8,128)(2,1)} %reshape_squeeze.9.hid_ref, f32[48,32]{1,0:T(8,128)} %bitcast.28, f32[4,3072]{1,0:T(4,128)} %bitcast.27, f32[4,8,24,128]{3,2,1,0:T(8,128)} %get-tuple-element.12.cos_ref, ...), custom_call_target="tpu_custom_call" | custom-call | tf_op jit(solution)/shard_map/pallas_call | solution.py:511
  111.0 1.8 %reshape.186 = bf16[1,12,4,3072]{3,2,1,0:T(4,128)(2,1)} reshape(bf16[48,3072]{1,0:T(8,128)(2,1)} %get-tuple-element.8) | data formatting | bytes 589824 | tf_op jit(solution)/shard_map/reshape | solution.py:578
  112.8 1.3 %copy.27 = f32[12,4,32]{2,1,0:T(4,128)} copy(f32[12,4,32]{2,1,0:T(4,128)} %bitcast.30) | data formatting | bytes 12288
  114.1 1.3 %copy.28 = f32[12,4,32]{2,1,0:T(4,128)} copy(f32[12,4,32]{2,1,0:T(4,128)} %bitcast.29) | data formatting | bytes 12288
  (3 shorter events, 0.0 us)

commit v2 on v1

v2 whole, which is shorter than its diff:
```python
import math

import jax
import jax.numpy as jnp
import numpy as np
from jax import lax
from jax.experimental import pallas as pl
from jax.experimental.pallas import tpu as pltpu
from jax.sharding import PartitionSpec as P

SIDE = 32
TXT = 512
STEPS = 28
EPSILON = 1e-06
ROPE_BASE = 10000.0
TIME_SHIFT = 3.0

MESH = pl.DeviceIdType.MESH
F32 = jnp.float32
BF16 = jnp.bfloat16

D = 3072
HALF = D // 2
HEAD = 128
UNITS = 768
PROMPTS = 4
RING = 4
TOKS = 8
MLPS = 16
PIECE = 24
CHUNK = RING * PIECE
STAGE = 2 * CHUNK
SLOTS = 192
ROWS_OWN = 2 * PIECE
MOD_COLS = 120
CH_HALF = 32


def sigma_at(position, steps_total):
    remain = 1.0 - position / steps_total
    return TIME_SHIFT * remain / (1.0 + (TIME_SHIFT - 1.0) * remain)


def layer_norm(values):
    average = jnp.mean(values, axis=-1, keepdims=True)
    centred = values - average
    spread = jnp.mean(centred * centred, axis=-1, keepdims=True)
    return centred * lax.rsqrt(spread + EPSILON)


def dot_f32(a, b):
    return jnp.dot(a, b, preferred_element_type=F32)


def dot_t(a, b):
    return lax.dot_general(a, b, (((1,), (1,)), ((), ())), preferred_element_type=F32)


def kernel(
    hid_ref, lat_ref, vec_ref, token_ref, len_ref, step_ref, guide_ref, gain_ref, place_ref, tab_ref,
    wmod_hbm, wqkv_hbm, wmi_hbm, wao_hbm, wmo_hbm, wfin_hbm,
    vel_ref, latn_ref, stream_ref,
    HID, TT, COS, SIN, MASK, IMAGE, GAIN, X, N, WMOD, WQKV, WMI, WAO, WMO, WFIN, G, MOD, QF, ST, R, OS, OR, ATT,
    ACT, ACC, PS, RB, RC, PS2, RB2, RC2, VS, VR,
    ag_s, ag_r, rs_s, rs_r, w_l, w_s, w_r, m_s, m_r, z_l, z_s, z_r, f_s, f_r, o_s, o_r, v_s, v_r,
):
    c = lax.axis_index("cfg")
    t = lax.axis_index("tok")
    m = lax.axis_index("mlp")
    x, y = m // RING, m % RING
    uv = ((x, y), (y, x))

    def at_uv(k, u, v):
        return u * RING + v if k == 0 else v * RING + u

    def remote(src, dst, ssem, rsem, **where):
        return pltpu.make_async_remote_copy(
            src_ref=src, dst_ref=dst, send_sem=ssem, recv_sem=rsem,
            device_id=where, device_id_type=MESH,
        )

    barrier = pltpu.get_barrier_semaphore()
    for d in range(1, MLPS):
        pl.semaphore_signal(barrier, inc=1, device_id={"mlp": (m + d) % MLPS}, device_id_type=MESH)
    for d in range(1, TOKS):
        pl.semaphore_signal(barrier, inc=1, device_id={"tok": (t + d) % TOKS}, device_id_type=MESH)
    pl.semaphore_signal(barrier, inc=1, device_id={"cfg": 1 - c}, device_id_type=MESH)

    wmod_copy = pltpu.make_async_copy(wmod_hbm, WMOD, w_l.at[0])
    wmod_copy.start()
    k_rows = pl.ds(pl.multiple_of(c * HALF, HALF), HALF)
    weights = (
        [(wqkv_hbm.at[j], WQKV.at[k_rows, pl.ds(j * HEAD, HEAD)]) for j in range(3)]
        + [(wmi_hbm, WMI.at[k_rows]), (wao_hbm, WAO.at[c]), (wmo_hbm, WMO.at[c])]
    )
    local_w = [pltpu.make_async_copy(s, d, w_l.at[1 + i]) for i, (s, d) in enumerate(weights)]
    remote_w = [remote(s, d, w_s.at[i], w_r.at[i], cfg=1 - c) for i, (s, d) in enumerate(weights)]
    fin_copy = pltpu.make_async_copy(wfin_hbm, WFIN, w_l.at[7])

    for i in range(ROWS_OWN // PROMPTS):
        HID[i * PROMPTS : (i + 1) * PROMPTS, :] = hid_ref[i].astype(F32)
    normed = layer_norm(HID[...]).astype(BF16)
    X[0, y, x] = normed[:PIECE]
    X[1, x, y] = normed[PIECE:]

    vec = vec_ref[...]
    silu_vec = (vec * (1.0 / (1.0 + jnp.exp(-vec)))).astype(BF16)
    wmod_copy.wait()
    G[t, m, :, 0:MOD_COLS] = dot_t(silu_vec, WMOD[...])
    pl.semaphore_wait(barrier, MLPS - 1 + TOKS - 1 + 1)
    mod1 = [
        remote(G.at[t, m], G.at[t, m], m_s.at[0], m_r.at[0], mlp=(m + d) % MLPS) for d in range(1, MLPS)
    ]
    for copy in mod1:
        copy.start()

    lo, hi = pl.ds(0, HALF), pl.ds(HALF, HALF)

    def order_u(u, j):
        return (u, (u + 3) % RING, (u + 1) % RING, (u + 2) % RING)[j]

    def ag(k, i):
        u, v = uv[k]
        sems = (ag_s.at[k, i], ag_r.at[k, i])
        up, um = {"mlp": at_uv(k, (u + 1) % RING, v)}, {"mlp": at_uv(k, (u + 3) % RING, v)}
        vp, vm = {"mlp": at_uv(k, u, (v + 1) % RING)}, {"mlp": at_uv(k, u, (v + 3) % RING)}
        if i < 2:
            block = X.at[k, v, u]
            return remote(block, block, *sems, **(up if i == 0 else um))
        if i < 4:
            block = X.at[k, v, (u + (3 if i == 2 else 1)) % RING, :, lo if i == 2 else hi]
            return remote(block, block, *sems, **(up if i == 2 else um))
        if i < 12:
            j, d = (i - 4) // 2, (i - 4) % 2
            block = X.at[k, v, order_u(u, j)]
            return remote(block, block, *sems, **(vp if d == 0 else vm))
        j, d = (i - 12) // 2, (i - 12) % 2
        block = X.at[k, (v + (3 if d == 0 else 1)) % RING, order_u(u, j), :, lo if d == 0 else hi]
        return remote(block, block, *sems, **(vp if d == 0 else vm))

    def ag_start(ids):
        for i in ids:
            for k in range(2):
                ag(k, i).start()

    def ag_recv(ids):
        for i in ids:
            for k in range(2):
                ag(k, i).wait_recv()

    ag_start((0, 1))
    for copy in local_w[:3]:
        copy.start()
    for copy in remote_w[:3]:
        copy.start()
    for i in range(3, 6):
        local_w[i].start()
        remote_w[i].start()
    fin_copy.start()
    ag_start((4, 5))

    tokens = token_ref[...]
    is_image = tokens >= TXT
    place = jnp.where(is_image, tokens - TXT, 0)
    TT[0:4, :] = (place // SIDE).astype(F32)
    TT[4:8, :] = (place % SIDE).astype(F32)
    TT[8:12, :] = jnp.where(is_image, 1.0, 0.0)
    TT[12:16, :] = jnp.zeros((4, TOKS * SLOTS), F32)
    kinds = TT[...].astype(BF16)

    def lanes(shape):
        return lax.broadcasted_iota(jnp.int32, shape, 1)

    place_x = (place_ref[:, 0:1] + x) % RING
    place_y = (place_ref[:, 1:2] + y) % RING
    natural = (RING * place_x + place_y) * (ROWS_OWN // PROMPTS) + place_ref[:, 2:3]
    chosen = jnp.where(lanes((SLOTS, TOKS * SLOTS)) == natural + t * SLOTS, 1.0, 0.0).astype(BF16)
    picked = dot_t(chosen, kinds)
    lane192 = lanes((SLOTS, SLOTS))
    for p in range(PROMPTS):
        wanted_pos = jnp.where(lane192 % 64 < 32, picked[:, p : p + 1], picked[:, 4 + p : 5 + p])
        hot = jnp.where((lane192 % 32).astype(F32) == wanted_pos, 1.0, 0.0).astype(BF16)
        both = dot_f32(hot, tab_ref[...])
        COS[p] = both[:, :HEAD].reshape(2 * RING, PIECE, HEAD)
        SIN[p] = both[:, HEAD:].reshape(2 * RING, PIECE, HEAD)
    sub = lax.broadcasted_iota(jnp.int32, (ROWS_OWN, TOKS * SLOTS), 0)
    chosen = jnp.where(
        lanes((ROWS_OWN, TOKS * SLOTS)) == sub // PROMPTS + (t * MLPS + m) * (ROWS_OWN // PROMPTS), 1.0, 0.0
    ).astype(BF16)
    sub16 = lax.broadcasted_iota(jnp.int32, (ROWS_OWN, 16), 0)
    own_image = jnp.where(lanes((ROWS_OWN, 16)) == 8 + sub16 % PROMPTS, dot_t(chosen, kinds), 0.0)
    IMAGE[...] = jnp.broadcast_to(jnp.sum(own_image, axis=-1, keepdims=True), (ROWS_OWN, CH_HALF))
    this = lax.broadcasted_iota(jnp.int32, (PROMPTS, TOKS * SLOTS), 0) == t // 2
    job_tokens = jnp.sum(jnp.where(this, tokens.astype(F32), 0.0), axis=0, keepdims=True)
    job_len = jnp.sum(
        jnp.where(lanes((1, PROMPTS)) == t // 2, len_ref[...].astype(F32), 0.0), axis=-1, keepdims=True
    )
    valid = jnp.where((job_tokens >= TXT) | (job_tokens < job_len), 1.0, 0.0)
    valid = jnp.concatenate([valid[:, i * SLOTS : (i + 1) * SLOTS] for i in range(TOKS)], axis=0)
    valid = dot_t(valid.astype(BF16), jnp.where(lane192 == natural, 1.0, 0.0).astype(BF16))
    MASK[...] = jnp.concatenate([valid[i : i + 1, :] for i in range(TOKS)], axis=1)

    ag_recv((0, 1))
    ag_start((2, 3, 6, 7, 8, 9))

    span1 = remote(G.at[t, pl.ds(0, MLPS - 1)], G.at[t, pl.ds(0, MLPS - 1)], m_s.at[0], m_r.at[0], mlp=(m + 1) % MLPS)
    span1.wait_recv()
    mod2 = [remote(G.at[t], G.at[t], m_s.at[1], m_r.at[1], tok=(t + d) % TOKS) for d in range(1, TOKS)]
    for copy in mod2:
        copy.start()

    ag_recv((2, 3))
    ag_start((10, 11))

    for copy in local_w[:3]:
        copy.wait()
    for copy in remote_w[:3]:
        copy.wait_recv()
    src_col = lax.broadcasted_iota(jnp.int32, (HEAD, HEAD), 0)
    out_col = lax.broadcasted_iota(jnp.int32, (HEAD, HEAD), 1)
    wanted = jnp.where(out_col < HEAD // 2, 2 * out_col, 2 * out_col - HEAD + 1)
    permute = jnp.where(src_col == wanted, 1.0, 0.0).astype(BF16)

    gain = gain_ref[...]
    gain_sum = jnp.zeros((2, HEAD), F32)
    for _ in range(3):
        part = gain.astype(BF16)
        gain_sum = gain_sum + dot_f32(part, permute)
        gain = gain - part.astype(F32)
    GAIN[...] = gain_sum

    def permute_step(i, carry):
        rows = pl.ds(pl.multiple_of(i * 512, 512), 512)
        for j in range(2):
            cols = pl.ds(j * HEAD, HEAD)
            WQKV[rows, cols] = dot_f32(WQKV[rows, cols], permute).astype(BF16)
        return carry

    lax.fori_loop(0, D // 512, permute_step, 0)

    span2 = remote(
        G.at[pl.ds(0, TOKS - 1)], G.at[pl.ds(0, TOKS - 1)], m_s.at[1], m_r.at[1], tok=(t + 1) % TOKS
    )
    span2.wait_recv()
    lane = lax.broadcasted_iota(jnp.int32, (PROMPTS, 128), 1)

    def mod_step(i, carry):
        base = pl.multiple_of(i * (MLPS * MOD_COLS), 128)
        for j in range(15):
            shift = (8 * j) % MOD_COLS
            first = G[i, j]
            if shift:
                first = pltpu.roll(first, 128 - shift, 1)
            second = pltpu.roll(G[i, j + 1], MOD_COLS - shift, 1)
            both = jnp.where(lane < MOD_COLS - shift, first, second)
            MOD[:, pl.ds(base + j * 128, 128)] = jnp.concatenate([both, both], axis=0)
        return carry

    lax.fori_loop(0, TOKS, mod_step, 0)

    for i in range(3, 4):
        local_w[i].wait()
        remote_w[i].wait_recv()

    batches = [[(k, 0, j) for k in range(2) for j in range(RING)]]
    batches += [[(k, dv, j) for k in range(2) for dv in (1, 3)] for j in range(RING)]
    batches += [[(k, 2, j) for half in range(2) for k in range(2) for j in (2 * half, 2 * half + 1)]]
    starts = (0, 192, 288, 384, 480, 576)

    def modulate(b):
        blocks = batches[b]

        def step(i, carry):
            cols = pl.ds(pl.multiple_of(i * 256, 256), 256)
            scale = 1.0 + MOD[:, pl.ds(pl.multiple_of(D + i * 256, 256), 256)]
            shift = MOD[:, cols]
            for pair in range(0, len(blocks), 2):
                pieces = [
                    X[k, (uv[k][1] + dv) % RING, order_u(uv[k][0], j), :, cols].astype(F32).reshape(3, 8, 256)
                    for k, dv, j in blocks[pair : pair + 2]
                ]
                both = jnp.concatenate(pieces, axis=0) * scale[None] + shift[None]
                first = starts[b] + pair * PIECE
                N[first : first + 48, cols] = both.reshape(48, 256).astype(BF16)
            return carry

        lax.fori_loop(0, D // 256, step, 0)

    soft_scale = math.log2(math.e) / math.sqrt(HEAD)

    def groups_of(b):
        return len(batches[b]) // RING, starts[b] // CHUNK

    def qkv(b):
        count, g0 = groups_of(b)
        rows_b = count * CHUNK
        pre = dot_f32(N[starts[b] : starts[b] + rows_b, :], WQKV[...])
        for j in range(3):
            QF[j, 0:rows_b] = pre[:, j * HEAD : (j + 1) * HEAD]
        for p in range(PROMPTS):
            rows = pl.ds(p, count * PIECE, stride=PROMPTS)
            cosine = COS[p, g0 : g0 + count].reshape(count * PIECE, HEAD)
            sine = SIN[p, g0 : g0 + count].reshape(count * PIECE, HEAD)
            outs = []
            for j in range(2):
                val = QF.at[j][rows, :]
                val = val * lax.rsqrt(jnp.mean(val * val, axis=-1, keepdims=True) + EPSILON) * GAIN[j : j + 1, :]
                outs.append((val * cosine + pltpu.roll(val, HEAD // 2, 1) * sine).astype(BF16))
            outs.append(QF.at[2][rows, :].astype(BF16))
            for place, val in ((0, outs[1]), (1, outs[2]), (2, outs[0])):
                for g in range(count):
                    ST[p, g0 + g, place] = val[g * PIECE : (g + 1) * PIECE]

    def job(i):
        p = (t // 2 + i) % PROMPTS
        rel = (t - 2 * p + TOKS) % TOKS
        half = 1 - ((rel + 7) % TOKS) // RING
        return p, 2 * p + half

    sign = 1 - 2 * (t % 2)
    partner = t + sign
    kv = pl.ds(0, 2)

    def tile(o):
        return (t + TOKS - sign * o) % TOKS

    def z_local(b):
        count, g0 = groups_of(b)
        gs = pl.ds(g0, count)
        return pltpu.make_async_copy(ST.at[t // 2, gs], R.at[t, gs], z_l.at[b])

    def z_send(b, i):
        count, g0 = groups_of(b)
        gs = pl.ds(g0, count)
        p, z_query = job(i)
        return remote(ST.at[p, gs], R.at[t, gs], z_s.at[i, b], z_r.at[t, b], tok=z_query)

    def z_near(b, o):
        count, g0 = groups_of(b)
        block = R.at[tile(o), pl.ds(g0, count)]
        return remote(block, block, z_s.at[0, b], z_r.at[tile(o), b], tok=partner)

    def z_hand(b, o):
        count, g0 = groups_of(b)
        gs = pl.ds(g0, count)
        src = ST.at[t // 2, gs, kv] if o == 0 else R.at[tile(o), gs, kv]
        return remote(src, R.at[tile(o), gs, kv], f_s.at[o, b], f_r.at[tile(o), b], tok=partner)

    def z_far(b, o):
        count, g0 = groups_of(b)
        block = R.at[tile(o), pl.ds(g0, count), kv]
        return remote(block, block, f_s.at[0, b], f_r.at[tile(o), b], tok=partner)

    def send_batch(b):
        for i in (2, 1, 3):
            z_send(b, i).start()
        z_local(b).start()
        z_hand(b, 0).start()

    def hand_on(b):
        for o in range(1, RING):
            z_near(b, o).wait_recv()
            z_hand(b, o).start()

    def units(first, count):
        def step(i, carry):
            cols = pl.ds(pl.multiple_of(i * 256, 256), 256)
            ACT[first : first + count, cols] = jax.nn.gelu(
                dot_f32(N[first : first + count, :], WMI[:, cols]), approximate=True
            ).astype(BF16)
            return carry

        lax.fori_loop(0, UNITS // 256, step, 0)

    def units_out(first, count):
        def step(i, carry):
            cols = pl.ds(pl.multiple_of(i * 256, 256), 256)
            for h in range(2):
                ACC[h, first : first + count, cols] = dot_f32(ACT[first : first + count, :], WMO[h, :, cols])
            return carry

        lax.fori_loop(0, HALF // 256, step, 0)

    def take(b):
        modulate(b)
        qkv(b)
        send_batch(b)

    take(0)
    ag_recv((4, 5))
    ag_start((12, 13))
    take(1)
    units(0, 192)
    ag_recv((6, 7))
    ag_start((14, 15))
    take(2)
    hand_on(0)
    hand_on(1)
    ag_recv((8, 9))
    ag_start((16, 17))
    take(3)
    hand_on(2)
    for i in range(4, 6):
        local_w[i].wait()
        remote_w[i].wait_recv()
    ag_recv((10, 11))
    ag_start((18, 19))
    take(4)
    hand_on(3)
    units(192, 192)
    hand_on(4)
    units_out(0, 192)
    ag_recv(range(12, 20))
    take(5)
    units(384, 192)
    hand_on(5)
    units(576, 192)
    units_out(192, 192)
    units_out(384, 192)
    units_out(576, 192)

    for b in range(len(batches)):
        z_local(b).wait()
        for o in range(RING, TOKS):
            z_far(b, o).wait_recv()
    own_p = t // 2

    def attend(o):
        keys = R[:, :, 0].reshape(TOKS * SLOTS, HEAD)
        vals = R[:, :, 1].reshape(TOKS * SLOTS, HEAD)
        query = R[tile(o), :, 2].reshape(SLOTS, HEAD)
        soft = jnp.exp2(dot_t(query, keys) * soft_scale) * MASK[...]
        total = jnp.sum(soft, axis=-1, keepdims=True)
        return (dot_f32(soft.astype(BF16), vals) / total).astype(BF16)

    for o in range(1, RING):
        OS[o] = attend(o)
        remote(OS.at[o], OR.at[own_p], o_s.at[o], o_r.at[own_p], tok=tile(o)).start()
    OR[own_p] = attend(0)

    for i in range(1, PROMPTS):
        p, z_query = job(i)
        remote(OS.at[0], OR.at[p], o_s.at[0], o_r.at[p], tok=z_query).wait_recv()
    for p in range(PROMPTS):
        ATT[pl.ds(p, SLOTS, stride=PROMPTS), :] = OR[p].astype(F32)

    rel_v = {0: 0, 1: 1, 3: 2, 2: 3}

    def out_rows(first, blocks):
        count = len(blocks) * PIECE
        att = ATT[first : first + count, :].astype(BF16)
        for h in range(2):
            for n in range(HALF // 512):
                cols = slice(n * 512, (n + 1) * 512)
                part = dot_f32(att, WAO[h, :, cols]) + ACC[h, first : first + count, cols]
                for i, (k, dv, j) in enumerate(blocks):
                    PS[k, rel_v[dv], j, :, h * HALF + n * 512 : h * HALF + (n + 1) * 512] = part[
                        i * PIECE : (i + 1) * PIECE
                    ].astype(BF16)

    def rs(k, i):
        u, v = uv[k]
        sems = (rs_s.at[k, i], rs_r.at[k, i])
        up, um = {"mlp": at_uv(k, (u + 1) % RING, v)}, {"mlp": at_uv(k, (u + 3) % RING, v)}
        vp, vm = {"mlp": at_uv(k, u, (v + 1) % RING)}, {"mlp": at_uv(k, u, (v + 3) % RING)}
        if i < 16:
            j, d = 3 - (i % 8) // 2, i % 2
            where = vp if d == 0 else vm
            if i < 8:
                block = PS.at[k, 3, j, :, lo if d == 0 else hi]
                return remote(block, RB.at[k, d, j], *sems, **where)
            block = PS.at[k, 1 + d, j]
            return remote(block, RC.at[k, d, j], *sems, **where)
        d = i % 2
        where = up if d == 0 else um
        if i < 18:
            return remote(PS2.at[k, 0, :, lo if d == 0 else hi], RB2.at[k, d], *sems, **where)
        return remote(PS2.at[k, 1 + d], RC2.at[k, d], *sems, **where)

    last = batches[5]
    for half in (1, 0):
        out_rows(576 + half * 96, last[half * 4 : half * 4 + 4])
        for i in range(4 * (1 - half), 4 * (1 - half) + 4):
            for k in range(2):
                rs(k, i).start()
    for step in range(RING):
        j = 3 - step
        out_rows(starts[1 + j], batches[1 + j])
        for d in range(2):
            for k in range(2):
                rs(k, 2 * step + d).wait_recv()
                cols = slice(0, HALF) if d == 0 else slice(HALF, D)
                PS[k, 1 + d, j, :, cols] = (
                    PS[k, 1 + d, j, :, cols].astype(F32) + RB[k, d, j].astype(F32)
                ).astype(BF16)
                rs(k, 8 + 2 * step + d).start()
    out_rows(0, batches[0])

    def own_sum(k, j):
        for d in range(2):
            rs(k, 8 + 2 * (3 - j) + d).wait_recv()
        return PS[k, 0, j].astype(F32) + RC[k, 0, j].astype(F32) + RC[k, 1, j].astype(F32)

    for k in range(2):
        PS2[k, 0] = own_sum(k, 3).astype(BF16)
        rs(k, 16).start()
        rs(k, 17).start()
    for d in range(2):
        for k in range(2):
            total = own_sum(k, 2 - d)
            rs(k, 16 + d).wait_recv()
            cols = slice(0, HALF) if d == 0 else slice(HALF, D)
            PS2[k, 1 + d] = total.astype(BF16)
            PS2[k, 1 + d, :, cols] = (total[:, cols] + RB2[k, d].astype(F32)).astype(BF16)
            rs(k, 18 + d).start()
    fin_copy.wait()
    finals = []
    for k in range(2):
        branch = own_sum(k, 0)
        for d in range(2):
            rs(k, 18 + d).wait_recv()
        branch = branch + RC2[k, 0].astype(F32) + RC2[k, 1].astype(F32)
        rows = slice(k * PIECE, (k + 1) * PIECE)
        gated = branch.reshape(3, 8, D) * MOD[:, 2 * D : 3 * D][None]
        stream = (HID[rows, :] + gated.reshape(PIECE, D)).astype(BF16)
        stream32 = stream.astype(F32)
        for i in range(PIECE // PROMPTS):
            stream_ref[k * (PIECE // PROMPTS) + i] = stream32[i * PROMPTS : (i + 1) * PROMPTS].astype(BF16)
        shaped = layer_norm(stream32).reshape(3, 8, D)
        shaped = shaped * (1.0 + MOD[:, 4 * D : 5 * D])[None] + MOD[:, 3 * D : 4 * D][None]
        finals.append(shaped.reshape(PIECE, D).astype(BF16).astype(F32))
    final_normed = jnp.concatenate(finals, axis=0).astype(BF16)
    half_velocity = dot_t(final_normed, WFIN[...])
    parts = (half_velocity[:, :CH_HALF] * IMAGE[...], half_velocity[:, CH_HALF:] * IMAGE[...])
    first = c == 0
    VS[...] = jnp.where(first, parts[1], parts[0])
    swap = remote(VS, VR, v_s, v_r, cfg=1 - c)
    swap.start()
    own = jnp.where(first, parts[0], parts[1])
    swap.wait_recv()
    other = VR[...]
    cond = jnp.where(first, own, other)
    uncond = jnp.where(first, other, own)
    velocity = uncond + guide_ref[...] * (cond - uncond)
    current = step_ref[...].astype(F32)
    step_size = sigma_at(current + 1.0, STEPS) - sigma_at(current, STEPS)
    moved = step_size * velocity
    for i in range(ROWS_OWN // PROMPTS):
        rows = slice(i * PROMPTS, (i + 1) * PROMPTS)
        vel_ref[i] = velocity[rows]
        latn_ref[i] = lat_ref[i] + moved[rows]

    swap.wait_send()
    for copy in remote_w:
        copy.wait_send()
    span1.wait_send()
    span2.wait_send()
    for k in range(2):
        for i in range(20):
            ag(k, i).wait_send()
            rs(k, i).wait_send()
    for b in range(len(batches)):
        for i in range(1, PROMPTS):
            z_send(b, i).wait_send()
        for o in range(RING):
            z_hand(b, o).wait_send()
    for o in range(1, RING):
        remote(OS.at[o], OR.at[own_p], o_s.at[o], o_r.at[own_p], tok=tile(o)).wait_send()


def call_kernel(*operands):
    vmem = pl.BlockSpec(memory_space=pltpu.VMEM)
    hbm = pl.BlockSpec(memory_space=pl.ANY)
    dma = pltpu.SemaphoreType.DMA
    scratch = [
        pltpu.VMEM((ROWS_OWN, D), F32),
        pltpu.VMEM((16, TOKS * SLOTS), F32),
        pltpu.VMEM((PROMPTS, 2 * RING, PIECE, HEAD), F32),
        pltpu.VMEM((PROMPTS, 2 * RING, PIECE, HEAD), F32),
        pltpu.VMEM((1, TOKS * SLOTS), F32),
        pltpu.VMEM((ROWS_OWN, CH_HALF), F32),
        pltpu.VMEM((2, HEAD), F32),
        pltpu.VMEM((2, RING, RING, PIECE, D), BF16),
        pltpu.VMEM((PROMPTS * SLOTS, D), BF16),
        pltpu.VMEM((MOD_COLS, D), BF16),
        pltpu.VMEM((D, 3 * HEAD), BF16),
        pltpu.VMEM((D, UNITS), BF16),
        pltpu.VMEM((2, HEAD, HALF), BF16),
        pltpu.VMEM((2, UNITS, HALF), BF16),
        pltpu.VMEM((2 * CH_HALF, D), BF16),
        pltpu.VMEM((TOKS, MLPS, PROMPTS, 128), F32),
        pltpu.VMEM((8, 5 * D), F32),
        pltpu.VMEM((3, STAGE, HEAD), F32),
        pltpu.VMEM((PROMPTS, 2 * RING, 3, PIECE, HEAD), BF16),
        pltpu.VMEM((TOKS, 2 * RING, 3, PIECE, HEAD), BF16),
        pltpu.VMEM((RING, SLOTS, HEAD), BF16),
        pltpu.VMEM((PROMPTS, SLOTS, HEAD), BF16),
        pltpu.VMEM((PROMPTS * SLOTS, HEAD), F32),
        pltpu.VMEM((PROMPTS * SLOTS, UNITS), BF16),
        pltpu.VMEM((2, PROMPTS * SLOTS, HALF), F32),
        pltpu.VMEM((2, RING, RING, PIECE, D), BF16),
        pltpu.VMEM((2, 2, RING, PIECE, HALF), BF16),
        pltpu.VMEM((2, 2, RING, PIECE, D), BF16),
        pltpu.VMEM((2, 3, PIECE, D), BF16),
        pltpu.VMEM((2, 2, PIECE, HALF), BF16),
        pltpu.VMEM((2, 2, PIECE, D), BF16),
        pltpu.VMEM((ROWS_OWN, CH_HALF), F32),
        pltpu.VMEM((ROWS_OWN, CH_HALF), F32),
        dma((2, 20)), dma((2, 20)), dma((2, 20)), dma((2, 20)),
        dma((8,)), dma((6,)), dma((6,)), dma((2,)), dma((2,)),
        dma((6,)), dma((PROMPTS, 6)), dma((TOKS, 6)), dma((RING, 6)), dma((TOKS, 6)),
        dma((RING,)), dma((PROMPTS,)), dma, dma,
    ]
    return pl.pallas_call(
        kernel,
        out_shape=(
            jax.ShapeDtypeStruct((ROWS_OWN // PROMPTS, PROMPTS, CH_HALF), F32),
            jax.ShapeDtypeStruct((ROWS_OWN // PROMPTS, PROMPTS, CH_HALF), F32),
            jax.ShapeDtypeStruct((ROWS_OWN // PROMPTS, PROMPTS, D), BF16),
        ),
        in_specs=[vmem] * 10 + [hbm] * 6,
        out_specs=(vmem, vmem, vmem),
        scratch_shapes=scratch,
        compiler_params=pltpu.CompilerParams(
            collective_id=0, has_side_effects=True, vmem_limit_bytes=67043328
        ),
    )(*operands)


def slot_places():
    blocks = [(k, 0, j) for k in range(2) for j in range(RING)]
    blocks += [(k, dv, j) for j in range(RING) for k in range(2) for dv in (1, 3)]
    blocks += [(k, 2, j) for half in range(2) for k in range(2) for j in (2 * half, 2 * half + 1)]
    rows = []
    for k, dv, j in blocks:
        du = (0, 3, 1, 2)[j]
        dx, dy = (du, dv) if k == 0 else (dv, du)
        rows += [(dx, dy, 6 * k + i) for i in range(6)]
    return np.array(rows, np.int32)


def rope_table():
    pairs = HEAD // 2
    first_pairs = HEAD // 16
    axis_pairs = (HEAD - HEAD // 8) // 4
    index = np.arange(pairs, dtype=np.float32)
    in_rows = (index >= first_pairs) & (index < first_pairs + axis_pairs)
    in_cols = index >= first_pairs + axis_pairs
    log_base = np.float32(math.log(ROPE_BASE))
    table = np.zeros((2 * SIDE, 2 * HEAD), np.float32)
    for pos in range(SIDE):
        for base, inside, start in ((0, in_rows, first_pairs), (SIDE, in_cols, first_pairs + axis_pairs)):
            freq = np.exp(-log_base * (index - np.float32(start)) / np.float32(axis_pairs)).astype(np.float32)
            angle = np.where(inside, np.float32(pos) * freq, 0.0).astype(np.float32)
            still = ~(in_rows | in_cols) if base == 0 else np.zeros_like(inside)
            cosine = np.where(inside, np.cos(angle), np.where(still, 1.0, 0.0))
            sine = np.where(inside, np.sin(angle), 0.0)
            table[base + pos] = np.concatenate([cosine, cosine, -sine, sine])
    parts, left = [], table
    for _ in range(3):
        part = left.astype(jnp.bfloat16)
        parts.append(part)
        left = left - part.astype(np.float32)
    return np.concatenate(parts, axis=0)


def on_device(
    hidden, latents, vec, slot_token, text_len, step_index, guidance,
    w_mod, w_qkv, w_mlp_in, qk_gain, w_attn_out, w_mlp_out, w_final,
):
    velocity, latents_next, stream = call_kernel(
        hidden[0], latents, vec[0], slot_token, text_len, step_index[None], guidance[None], qk_gain[0],
        jnp.asarray(slot_places()), jnp.asarray(rope_table()),
        w_mod.T, w_qkv[0].transpose(1, 0, 2), w_mlp_in[0], w_attn_out[0], w_mlp_out[0], w_final.T,
    )
    return velocity, latents_next, stream[None]


def solution(mesh):
    return jax.shard_map(
        on_device,
        mesh=mesh,
        in_specs=(
            P("cfg", ("tok", "mlp"), None, None),
            P(("tok", "mlp"), None, "cfg"),
            P("cfg", None, None),
            P(),
            P("cfg", None),
            P(),
            P(),
            P(None, ("tok", "mlp")),
            P(None, "cfg", None, "mlp"),
            P(None, "cfg", "mlp"),
            P(),
            P(None, "mlp", "cfg"),
            P(None, "mlp", "cfg"),
            P(),
        ),
        out_specs=(
            P(("tok", "mlp"), None, "cfg"),
            P(("tok", "mlp"), None, "cfg"),
            P("cfg", ("tok", "mlp"), None, None),
        ),
        check_vma=False,
    )
```

time: 116 us -> 100 us (0.86)
  local copies, waits for them, and re-layouts: 14.3 us -> 4.47 us
  other arithmetic: 4.58 us -> 0 us
    reshape x4 -> x0, local copies, waits for them, and re-layouts: 4.22 us -> none  [the longest x1 1.79 us: on_device(): stream.reshape(hidden.shape)]
    mul x1 -> x0, other arithmetic: 2.87 us -> none  [rope_tables(): return (jnp.cos(angles), jnp.sin(angles) * side)]
    another operation x3 -> x0, local copies, waits for them, and re-layouts: 2.8 us -> none  [the longest x1 1.74 us: on_device(): hidden[0].reshape(ROWS_OWN, D)]
    unnamed x2 -> x3, local copies, waits for them, and re-layouts: 2.69 us -> 4.47 us
    convert_element_type x3 -> x0, other arithmetic: 1.52 us -> none  [the longest x1 0.77 us: on_device(): (own_tokens >= TXT).astype(F32)]
    broadcast_in_dim x2 -> x0, local copies, waits for them, and re-layouts: 1.33 us -> none  [the longest x1 0.69 us: on_device(): jnp.broadcast_to((own_tokens >= TXT).astype(F32), (ROWS_OWN, CH_HALF))]
    dynamic_slice x1 -> x0, local copies, waits for them, and re-layouts: 1.24 us -> none  [on_device(): lax.dynamic_index_in_dim(text_len[0], own_prompt, 0, keepdims=False)]
where the time goes in v2:
time: 100 us; the launch traced here: 99.8 us
  Pallas kernels  93.4 us (93%)
  local copies, waits for them, and re-layouts  4.47 us (4%)
  between operations  1.94 us (2%)
    pallas_call x1, Pallas kernels, call_kernel(): pl.pallas_call(kernel, out_shape=(jax.ShapeDtypeStruct((ROWS_OWN // PROMP...  93.4 us
    unnamed x3, local copies, waits for them, and re-layouts  4.47 us

profile of v2, /device:TPU:1, one launch (start us, length us, event | category | flops | bytes accessed | tf_op | source)
XLA Modules:
  0.0 99.8 jit_solution(3633876425190814870)
XLA Ops:
  1.9 93.4 %shard_map.175 = (f32[12,4,32]{2,1,0:T(4,128)}, f32[12,4,32]{2,1,0:T(4,128)}, bf16[12,4,3072]{2,1,0:T(4,128)(2,1)}) custom-call(bf16[12,4,3072]{2,1,0:T(4,128)(2,1)} %bitcast.22, f32[12,4,32]{2,1,0:T(4,128)} %lat_ref.1, f32[4,3072]{1,0:T(4,128)} %bitcast.24, s32[4,1536]{1,0:T(4,128)} %token_ref.1, s32[1,4]{1,0:T(1,128)} %len_ref.1, ...), custom_call_target="tpu_custom_call" | custom-call | tf_op jit(solution)/shard_map/pallas_call | solution.py:614
  95.3 1.3 %copy.24 = f32[12,4,32]{2,1,0:T(4,128)} copy(f32[12,4,32]{2,1,0:T(4,128)} %get-tuple-element.12) | data formatting | bytes 12288
  96.7 1.3 %copy.25 = f32[12,4,32]{2,1,0:T(4,128)} copy(f32[12,4,32]{2,1,0:T(4,128)} %get-tuple-element.13) | data formatting | bytes 12288
  98.0 1.8 %copy.26 = bf16[1,12,4,3072]{3,2,1,0:T(4,128)(2,1)} copy(bf16[1,12,4,3072]{3,2,1,0:T(4,128)(2,1)} %bitcast.23) | data formatting | bytes 589824

commit v3 on v2

--- a/solution.py
+++ b/solution.py
@@ -57,9 +57,9 @@
 
 
 def kernel(
-    hid_ref, lat_ref, vec_ref, token_ref, len_ref, step_ref, guide_ref, gain_ref, place_ref, tab_ref,
+    hid_ref, vec_ref, token_ref, len_ref, gain_ref, place_ref, tab_ref,
     wmod_hbm, wqkv_hbm, wmi_hbm, wao_hbm, wmo_hbm, wfin_hbm,
-    vel_ref, latn_ref, stream_ref,
+    cond_ref, uncond_ref, stream_ref,
     HID, TT, COS, SIN, MASK, IMAGE, GAIN, X, N, WMOD, WQKV, WMI, WAO, WMO, WFIN, G, MOD, QF, ST, R, OS, OR, ATT,
     ACT, ACC, PS, RB, RC, PS2, RB2, RC2, VS, VR,
     ag_s, ag_r, rs_s, rs_r, w_l, w_s, w_r, m_s, m_r, z_l, z_s, z_r, f_s, f_r, o_s, o_r, v_s, v_r,
@@ -148,7 +148,8 @@
             for k in range(2):
                 ag(k, i).wait_recv()
 
-    ag_start((0, 1))
+    ag_start((0, 1, 4, 5))
+
     for copy in local_w[:3]:
         copy.start()
     for copy in remote_w[:3]:
@@ -157,7 +158,6 @@
         local_w[i].start()
         remote_w[i].start()
     fin_copy.start()
-    ag_start((4, 5))
 
     tokens = token_ref[...]
     is_image = tokens >= TXT
@@ -252,7 +252,9 @@
             if shift:
                 first = pltpu.roll(first, 128 - shift, 1)
             second = pltpu.roll(G[i, j + 1], MOD_COLS - shift, 1)
-            both = jnp.where(lane < MOD_COLS - shift, first, second)
+            index = i * 15 + j
+            is_scale = jnp.where(((index >= 24) & (index < 48)) | (index >= 96), 1.0, 0.0)
+            both = jnp.where(lane < MOD_COLS - shift, first, second) + is_scale
             MOD[:, pl.ds(base + j * 128, 128)] = jnp.concatenate([both, both], axis=0)
         return carry
 
@@ -264,27 +266,28 @@
 
     batches = [[(k, 0, j) for k in range(2) for j in range(RING)]]
     batches += [[(k, dv, j) for k in range(2) for dv in (1, 3)] for j in range(RING)]
-    batches += [[(k, 2, j) for half in range(2) for k in range(2) for j in (2 * half, 2 * half + 1)]]
-    starts = (0, 192, 288, 384, 480, 576)
+    batches += [[(k, 2, j) for k in range(2) for j in (2 * half, 2 * half + 1)] for half in range(2)]
+    starts = (0, 192, 288, 384, 480, 576, 672)
+    width = 768
 
     def modulate(b):
         blocks = batches[b]
 
         def step(i, carry):
-            cols = pl.ds(pl.multiple_of(i * 256, 256), 256)
-            scale = 1.0 + MOD[:, pl.ds(pl.multiple_of(D + i * 256, 256), 256)]
+            cols = pl.ds(pl.multiple_of(i * width, width), width)
+            scale = MOD[:, pl.ds(pl.multiple_of(D + i * width, width), width)]
             shift = MOD[:, cols]
             for pair in range(0, len(blocks), 2):
                 pieces = [
-                    X[k, (uv[k][1] + dv) % RING, order_u(uv[k][0], j), :, cols].astype(F32).reshape(3, 8, 256)
+                    X[k, (uv[k][1] + dv) % RING, order_u(uv[k][0], j), :, cols].astype(F32).reshape(3, 8, width)
                     for k, dv, j in blocks[pair : pair + 2]
                 ]
                 both = jnp.concatenate(pieces, axis=0) * scale[None] + shift[None]
                 first = starts[b] + pair * PIECE
-                N[first : first + 48, cols] = both.reshape(48, 256).astype(BF16)
+                N[first : first + 48, cols] = both.reshape(48, width).astype(BF16)
             return carry
 
-        lax.fori_loop(0, D // 256, step, 0)
+        lax.fori_loop(0, D // width, step, 0)
 
     soft_scale = math.log2(math.e) / math.sqrt(HEAD)
 
@@ -357,6 +360,13 @@
         z_local(b).start()
         z_hand(b, 0).start()
 
+    def z_both(b, i):
+        count, g0 = groups_of(b)
+        gs = pl.ds(g0, count)
+        p, z_query = job(i)
+        other = 4 * p + 1 - z_query
+        return remote(ST.at[p, gs, kv], R.at[t, gs, kv], f_s.at[i, b], f_r.at[t, b], tok=other)
+
     def hand_on(b):
         for o in range(1, RING):
             z_near(b, o).wait_recv()
@@ -389,35 +399,39 @@
     take(0)
     ag_recv((4, 5))
     ag_start((12, 13))
-    take(1)
-    units(0, 192)
     ag_recv((6, 7))
     ag_start((14, 15))
+    take(1)
     take(2)
-    hand_on(0)
-    hand_on(1)
+    units(0, 192)
     ag_recv((8, 9))
     ag_start((16, 17))
     take(3)
-    hand_on(2)
+    for b in range(3):
+        hand_on(b)
     for i in range(4, 6):
         local_w[i].wait()
         remote_w[i].wait_recv()
+    units_out(0, 192)
     ag_recv((10, 11))
     ag_start((18, 19))
     take(4)
     hand_on(3)
     units(192, 192)
+    ag_recv(range(12, 16))
+    take(5)
     hand_on(4)
-    units_out(0, 192)
-    ag_recv(range(12, 20))
-    take(5)
+    ag_recv(range(16, 20))
+    take(6)
+    for i in (2, 1, 3):
+        z_both(6, i).start()
+    hand_on(5)
     units(384, 192)
-    hand_on(5)
     units(576, 192)
-    units_out(192, 192)
-    units_out(384, 192)
+    units_out(192, 384)
     units_out(576, 192)
+    for o in range(1, RING):
+        z_near(6, o).wait_recv()
 
     for b in range(len(batches)):
         z_local(b).wait()
@@ -477,9 +491,8 @@
             return remote(PS2.at[k, 0, :, lo if d == 0 else hi], RB2.at[k, d], *sems, **where)
         return remote(PS2.at[k, 1 + d], RC2.at[k, d], *sems, **where)
 
-    last = batches[5]
     for half in (1, 0):
-        out_rows(576 + half * 96, last[half * 4 : half * 4 + 4])
+        out_rows(starts[5 + half], batches[5 + half])
         for i in range(4 * (1 - half), 4 * (1 - half) + 4):
             for k in range(2):
                 rs(k, i).start()
@@ -527,7 +540,7 @@
         for i in range(PIECE // PROMPTS):
             stream_ref[k * (PIECE // PROMPTS) + i] = stream32[i * PROMPTS : (i + 1) * PROMPTS].astype(BF16)
         shaped = layer_norm(stream32).reshape(3, 8, D)
-        shaped = shaped * (1.0 + MOD[:, 4 * D : 5 * D])[None] + MOD[:, 3 * D : 4 * D][None]
+        shaped = shaped * MOD[:, 4 * D : 5 * D][None] + MOD[:, 3 * D : 4 * D][None]
         finals.append(shaped.reshape(PIECE, D).astype(BF16).astype(F32))
     final_normed = jnp.concatenate(finals, axis=0).astype(BF16)
     half_velocity = dot_t(final_normed, WFIN[...])
@@ -541,14 +554,10 @@
     other = VR[...]
     cond = jnp.where(first, own, other)
     uncond = jnp.where(first, other, own)
-    velocity = uncond + guide_ref[...] * (cond - uncond)
-    current = step_ref[...].astype(F32)
-    step_size = sigma_at(current + 1.0, STEPS) - sigma_at(current, STEPS)
-    moved = step_size * velocity
     for i in range(ROWS_OWN // PROMPTS):
         rows = slice(i * PROMPTS, (i + 1) * PROMPTS)
-        vel_ref[i] = velocity[rows]
-        latn_ref[i] = lat_ref[i] + moved[rows]
+        cond_ref[i] = cond[rows]
+        uncond_ref[i] = uncond[rows]
 
     swap.wait_send()
     for copy in remote_w:
@@ -563,7 +572,7 @@
         for i in range(1, PROMPTS):
             z_send(b, i).wait_send()
         for o in range(RING):
-            z_hand(b, o).wait_send()
+            (z_both(b, o) if b == 6 and o else z_hand(b, o)).wait_send()
     for o in range(1, RING):
         remote(OS.at[o], OR.at[own_p], o_s.at[o], o_r.at[own_p], tok=tile(o)).wait_send()
 
@@ -608,7 +617,7 @@
         pltpu.VMEM((ROWS_OWN, CH_HALF), F32),
         dma((2, 20)), dma((2, 20)), dma((2, 20)), dma((2, 20)),
         dma((8,)), dma((6,)), dma((6,)), dma((2,)), dma((2,)),
-        dma((6,)), dma((PROMPTS, 6)), dma((TOKS, 6)), dma((RING, 6)), dma((TOKS, 6)),
+        dma((7,)), dma((PROMPTS, 7)), dma((TOKS, 7)), dma((RING, 7)), dma((TOKS, 7)),
         dma((RING,)), dma((PROMPTS,)), dma, dma,
     ]
     return pl.pallas_call(
@@ -618,7 +627,7 @@
             jax.ShapeDtypeStruct((ROWS_OWN // PROMPTS, PROMPTS, CH_HALF), F32),
             jax.ShapeDtypeStruct((ROWS_OWN // PROMPTS, PROMPTS, D), BF16),
         ),
-        in_specs=[vmem] * 10 + [hbm] * 6,
+        in_specs=[vmem] * 7 + [hbm] * 6,
         out_specs=(vmem, vmem, vmem),
         scratch_shapes=scratch,
         compiler_params=pltpu.CompilerParams(
@@ -668,12 +677,14 @@
     hidden, latents, vec, slot_token, text_len, step_index, guidance,
     w_mod, w_qkv, w_mlp_in, qk_gain, w_attn_out, w_mlp_out, w_final,
 ):
-    velocity, latents_next, stream = call_kernel(
-        hidden[0], latents, vec[0], slot_token, text_len, step_index[None], guidance[None], qk_gain[0],
-        jnp.asarray(slot_places()), jnp.asarray(rope_table()),
+    cond, uncond, stream = call_kernel(
+        hidden[0], vec[0], slot_token, text_len, qk_gain[0], jnp.asarray(slot_places()), jnp.asarray(rope_table()),
         w_mod.T, w_qkv[0].transpose(1, 0, 2), w_mlp_in[0], w_attn_out[0], w_mlp_out[0], w_final.T,
     )
-    return velocity, latents_next, stream[None]
+    velocity = uncond + guidance[0] * (cond - uncond)
+    current = step_index[0].astype(F32)
+    step_size = sigma_at(current + 1.0, STEPS) - sigma_at(current, STEPS)
+    return velocity, latents + step_size * velocity, stream[None]
 
 
 def solution(mesh):

time: 100 us -> 95.6 us (0.956)
  Pallas kernels: 93.4 us -> 90.1 us
  local copies, waits for them, and re-layouts: 4.47 us -> 1.78 us
  other arithmetic: 0 us -> 1.4 us
    pallas_call x1, Pallas kernels: 93.4 us -> 90.1 us  [call_kernel(): pl.pallas_call(kernel, out_shape=(jax.ShapeDtypeStruct((ROWS_OWN // PROMP...]
    unnamed x3 -> x1, local copies, waits for them, and re-layouts: 4.47 us -> 1.78 us
    add x0 -> x1, other arithmetic: none -> 1.4 us  [on_device(): return (velocity, latents + step_size * velocity, stream[None])]
where the time goes in v3:
time: 95.6 us; the launch traced here: 95.3 us
  Pallas kernels  90.1 us (94%)
  between operations  2.03 us (2%)
  local copies, waits for them, and re-layouts  1.78 us (2%)
  other arithmetic  1.4 us (1%)
    pallas_call x1, Pallas kernels, call_kernel(): pl.pallas_call(kernel, out_shape=(jax.ShapeDtypeStruct((ROWS_OWN // PROMP...  90.1 us

profile of v3, /device:TPU:1, one launch (start us, length us, event | category | flops | bytes accessed | tf_op | source)
XLA Modules:
  0.0 95.3 jit_solution(13699425251987206582)
XLA Ops:
  2.0 90.1 %shard_map.175 = (f32[12,4,32]{2,1,0:T(4,128)}, f32[12,4,32]{2,1,0:T(4,128)}, bf16[12,4,3072]{2,1,0:T(4,128)(2,1)}) custom-call(bf16[12,4,3072]{2,1,0:T(4,128)(2,1)} %bitcast.26, f32[4,3072]{1,0:T(4,128)} %bitcast.28, s32[4,1536]{1,0:T(4,128)} %token_ref.1, s32[1,4]{1,0:T(1,128)} %len_ref.1, f32[2,128]{1,0:T(2,128)} %bitcast.34, ...), custom_call_target="tpu_custom_call" | custom-call | tf_op jit(solution)/shard_map/pallas_call | solution.py:623
  92.1 1.4 %multiply_add_fusion = (f32[6,8,32]{2,1,0:T(8,128)}, f32[6,8,32]{2,1,0:T(8,128)}) fusion(f32[6,8,32]{2,1,0:T(8,128)} %bitcast.29, f32[]{:T(128)} %bitcast.11, f32[6,8,32]{2,1,0:T(8,128)} %bitcast.33, f32[6,8,32]{2,1,0:T(8,128)} %bitcast.32, f32[]{:T(128)} %bitcast.19), kind=kLoop, calls=%fused_computation | loop fusion | flops 7680 | bytes 30728 | tf_op jit(solution)/shard_map/add | solution.py:687
  93.5 1.8 %copy.22 = bf16[1,12,4,3072]{3,2,1,0:T(4,128)(2,1)} copy(bf16[1,12,4,3072]{3,2,1,0:T(4,128)(2,1)} %bitcast.27) | data formatting | bytes 589824

commit v4 on v3

--- a/solution.py
+++ b/solution.py
@@ -57,12 +57,12 @@
 
 
 def kernel(
-    hid_ref, vec_ref, token_ref, len_ref, gain_ref, place_ref, tab_ref,
+    hid_hbm, vec_hbm, token_hbm, len_hbm, gain_hbm, place_hbm, tab_hbm,
     wmod_hbm, wqkv_hbm, wmi_hbm, wao_hbm, wmo_hbm, wfin_hbm,
-    cond_ref, uncond_ref, stream_ref,
-    HID, TT, COS, SIN, MASK, IMAGE, GAIN, X, N, WMOD, WQKV, WMI, WAO, WMO, WFIN, G, MOD, QF, ST, R, OS, OR, ATT,
+    cond_ref, uncond_ref, stream_hbm,
+    hid_ref, vec_ref, token_ref, len_ref, gain_ref, place_ref, tab_ref, stream_ref, HID, TT, COS, SIN, MASK, IMAGE, GAIN, X, N, WMOD, WQKV, WMI, WAO, WMO, WFIN, G, MOD, QF, ST, R, OS, OR, ATT,
     ACT, ACC, PS, RB, RC, PS2, RB2, RC2, VS, VR,
-    ag_s, ag_r, rs_s, rs_r, w_l, w_s, w_r, m_s, m_r, z_l, z_s, z_r, f_s, f_r, o_s, o_r, v_s, v_r,
+    ag_s, ag_r, rs_s, rs_r, w_l, w_s, w_r, m_s, m_r, z_l, z_s, z_r, f_s, f_r, o_s, o_r, v_s, v_r, in_l, out_l,
 ):
     c = lax.axis_index("cfg")
     t = lax.axis_index("tok")
@@ -85,6 +85,16 @@
     for d in range(1, TOKS):
         pl.semaphore_signal(barrier, inc=1, device_id={"tok": (t + d) % TOKS}, device_id_type=MESH)
     pl.semaphore_signal(barrier, inc=1, device_id={"cfg": 1 - c}, device_id_type=MESH)
+
+    inputs = [
+        pltpu.make_async_copy(src, dst, in_l.at[i])
+        for i, (src, dst) in enumerate((
+            (hid_hbm, hid_ref), (vec_hbm, vec_ref), (token_hbm, token_ref), (len_hbm, len_ref),
+            (gain_hbm, gain_ref), (place_hbm, place_ref), (tab_hbm, tab_ref),
+        ))
+    ]
+    for copy in inputs:
+        copy.start()
 
     wmod_copy = pltpu.make_async_copy(wmod_hbm, WMOD, w_l.at[0])
     wmod_copy.start()
@@ -97,16 +107,18 @@
     remote_w = [remote(s, d, w_s.at[i], w_r.at[i], cfg=1 - c) for i, (s, d) in enumerate(weights)]
     fin_copy = pltpu.make_async_copy(wfin_hbm, WFIN, w_l.at[7])
 
+    inputs[0].wait()
     for i in range(ROWS_OWN // PROMPTS):
         HID[i * PROMPTS : (i + 1) * PROMPTS, :] = hid_ref[i].astype(F32)
     normed = layer_norm(HID[...]).astype(BF16)
     X[0, y, x] = normed[:PIECE]
     X[1, x, y] = normed[PIECE:]
 
+    inputs[1].wait()
     vec = vec_ref[...]
     silu_vec = (vec * (1.0 / (1.0 + jnp.exp(-vec)))).astype(BF16)
     wmod_copy.wait()
-    G[t, m, :, 0:MOD_COLS] = dot_t(silu_vec, WMOD[...])
+    G[t, m, :, 0:MOD_COLS] = dot_t(silu_vec, WMOD[...]).astype(BF16)
     pl.semaphore_wait(barrier, MLPS - 1 + TOKS - 1 + 1)
     mod1 = [
         remote(G.at[t, m], G.at[t, m], m_s.at[0], m_r.at[0], mlp=(m + d) % MLPS) for d in range(1, MLPS)
@@ -159,6 +171,8 @@
         remote_w[i].start()
     fin_copy.start()
 
+    for copy in inputs[2:]:
+        copy.wait()
     tokens = token_ref[...]
     is_image = tokens >= TXT
     place = jnp.where(is_image, tokens - TXT, 0)
@@ -248,10 +262,10 @@
         base = pl.multiple_of(i * (MLPS * MOD_COLS), 128)
         for j in range(15):
             shift = (8 * j) % MOD_COLS
-            first = G[i, j]
+            first = G[i, j].astype(F32)
             if shift:
                 first = pltpu.roll(first, 128 - shift, 1)
-            second = pltpu.roll(G[i, j + 1], MOD_COLS - shift, 1)
+            second = pltpu.roll(G[i, j + 1].astype(F32), MOD_COLS - shift, 1)
             index = i * 15 + j
             is_scale = jnp.where(((index >= 24) & (index < 48)) | (index >= 96), 1.0, 0.0)
             both = jnp.where(lane < MOD_COLS - shift, first, second) + is_scale
@@ -373,23 +387,18 @@
             z_hand(b, o).start()
 
     def units(first, count):
-        def step(i, carry):
-            cols = pl.ds(pl.multiple_of(i * 256, 256), 256)
-            ACT[first : first + count, cols] = jax.nn.gelu(
-                dot_f32(N[first : first + count, :], WMI[:, cols]), approximate=True
-            ).astype(BF16)
-            return carry
-
-        lax.fori_loop(0, UNITS // 256, step, 0)
+        ACT[first : first + count, :] = jax.nn.gelu(
+            dot_f32(N[first : first + count, :], WMI[...]), approximate=True
+        ).astype(BF16)
 
     def units_out(first, count):
         def step(i, carry):
-            cols = pl.ds(pl.multiple_of(i * 256, 256), 256)
+            cols = pl.ds(pl.multiple_of(i * 512, 512), 512)
             for h in range(2):
                 ACC[h, first : first + count, cols] = dot_f32(ACT[first : first + count, :], WMO[h, :, cols])
             return carry
 
-        lax.fori_loop(0, HALF // 256, step, 0)
+        lax.fori_loop(0, HALF // 512, step, 0)
 
     def take(b):
         modulate(b)
@@ -528,6 +537,7 @@
             rs(k, 18 + d).start()
     fin_copy.wait()
     finals = []
+    stream_copy = pltpu.make_async_copy(stream_ref, stream_hbm, out_l)
     for k in range(2):
         branch = own_sum(k, 0)
         for d in range(2):
@@ -542,6 +552,7 @@
         shaped = layer_norm(stream32).reshape(3, 8, D)
         shaped = shaped * MOD[:, 4 * D : 5 * D][None] + MOD[:, 3 * D : 4 * D][None]
         finals.append(shaped.reshape(PIECE, D).astype(BF16).astype(F32))
+    stream_copy.start()
     final_normed = jnp.concatenate(finals, axis=0).astype(BF16)
     half_velocity = dot_t(final_normed, WFIN[...])
     parts = (half_velocity[:, :CH_HALF] * IMAGE[...], half_velocity[:, CH_HALF:] * IMAGE[...])
@@ -559,6 +570,7 @@
         cond_ref[i] = cond[rows]
         uncond_ref[i] = uncond[rows]
 
+    stream_copy.wait()
     swap.wait_send()
     for copy in remote_w:
         copy.wait_send()
@@ -582,6 +594,14 @@
     hbm = pl.BlockSpec(memory_space=pl.ANY)
     dma = pltpu.SemaphoreType.DMA
     scratch = [
+        pltpu.VMEM((ROWS_OWN // PROMPTS, PROMPTS, D), BF16),
+        pltpu.VMEM((PROMPTS, D), F32),
+        pltpu.VMEM((PROMPTS, TOKS * SLOTS), jnp.int32),
+        pltpu.VMEM((1, PROMPTS), jnp.int32),
+        pltpu.VMEM((2, HEAD), F32),
+        pltpu.VMEM((SLOTS, 3), jnp.int32),
+        pltpu.VMEM((SLOTS, 2 * HEAD), BF16),
+        pltpu.VMEM((ROWS_OWN // PROMPTS, PROMPTS, D), BF16),
         pltpu.VMEM((ROWS_OWN, D), F32),
         pltpu.VMEM((16, TOKS * SLOTS), F32),
         pltpu.VMEM((PROMPTS, 2 * RING, PIECE, HEAD), F32),
@@ -597,7 +617,7 @@
         pltpu.VMEM((2, HEAD, HALF), BF16),
         pltpu.VMEM((2, UNITS, HALF), BF16),
         pltpu.VMEM((2 * CH_HALF, D), BF16),
-        pltpu.VMEM((TOKS, MLPS, PROMPTS, 128), F32),
+        pltpu.VMEM((TOKS, MLPS, PROMPTS, 128), BF16),
         pltpu.VMEM((8, 5 * D), F32),
         pltpu.VMEM((3, STAGE, HEAD), F32),
         pltpu.VMEM((PROMPTS, 2 * RING, 3, PIECE, HEAD), BF16),
@@ -618,7 +638,7 @@
         dma((2, 20)), dma((2, 20)), dma((2, 20)), dma((2, 20)),
         dma((8,)), dma((6,)), dma((6,)), dma((2,)), dma((2,)),
         dma((7,)), dma((PROMPTS, 7)), dma((TOKS, 7)), dma((RING, 7)), dma((TOKS, 7)),
-        dma((RING,)), dma((PROMPTS,)), dma, dma,
+        dma((RING,)), dma((PROMPTS,)), dma, dma, dma((7,)), dma,
     ]
     return pl.pallas_call(
         kernel,
@@ -627,8 +647,8 @@
             jax.ShapeDtypeStruct((ROWS_OWN // PROMPTS, PROMPTS, CH_HALF), F32),
             jax.ShapeDtypeStruct((ROWS_OWN // PROMPTS, PROMPTS, D), BF16),
         ),
-        in_specs=[vmem] * 7 + [hbm] * 6,
-        out_specs=(vmem, vmem, vmem),
+        in_specs=[hbm] * 13,
+        out_specs=(vmem, vmem, hbm),
         scratch_shapes=scratch,
         compiler_params=pltpu.CompilerParams(
             collective_id=0, has_side_effects=True, vmem_limit_bytes=67043328

time: 95.6 us -> 91.7 us (0.959)
  Pallas kernels: 90.1 us -> 86.2 us
    pallas_call x1, Pallas kernels: 90.1 us -> 86.2 us  [call_kernel(): pl.pallas_call(kernel, out_shape=(jax.ShapeDtypeStruct((ROWS_OWN // PROMP...]
where the time goes in v4:
time: 91.7 us; the launch traced here: 91.4 us
  Pallas kernels  86.2 us (94%)
  between operations  2.03 us (2%)
  local copies, waits for them, and re-layouts  1.78 us (2%)
  other arithmetic  1.4 us (2%)
    pallas_call x1, Pallas kernels, call_kernel(): pl.pallas_call(kernel, out_shape=(jax.ShapeDtypeStruct((ROWS_OWN // PROMP...  86.2 us

profile of v4, /device:TPU:1, one launch (start us, length us, event | category | flops | bytes accessed | tf_op | source)
XLA Modules:
  0.0 91.4 jit_solution(933864721240170094)
XLA Ops:
  2.0 86.2 %shard_map.175 = (f32[12,4,32]{2,1,0:T(4,128)}, f32[12,4,32]{2,1,0:T(4,128)}, bf16[12,4,3072]{2,1,0:T(4,128)(2,1)}) custom-call(bf16[12,4,3072]{2,1,0:T(4,128)(2,1)} %bitcast.26, f32[4,3072]{1,0:T(4,128)} %bitcast.28, s32[4,1536]{1,0:T(4,128)} %token_hbm.1, s32[1,4]{1,0:T(1,128)} %len_hbm.1, f32[2,128]{1,0:T(2,128)} %bitcast.34, ...), custom_call_target="tpu_custom_call" | custom-call | tf_op jit(solution)/shard_map/pallas_call | solution.py:643
  88.3 1.4 %multiply_add_fusion = (f32[6,8,32]{2,1,0:T(8,128)}, f32[6,8,32]{2,1,0:T(8,128)}) fusion(f32[6,8,32]{2,1,0:T(8,128)} %bitcast.29, f32[]{:T(128)} %bitcast.11, f32[6,8,32]{2,1,0:T(8,128)} %bitcast.33, f32[6,8,32]{2,1,0:T(8,128)} %bitcast.32, f32[]{:T(128)} %bitcast.19), kind=kLoop, calls=%fused_computation | loop fusion | flops 7680 | bytes 30728 | tf_op jit(solution)/shard_map/add | solution.py:707
  89.7 1.8 %copy.22 = bf16[1,12,4,3072]{3,2,1,0:T(4,128)(2,1)} copy(bf16[1,12,4,3072]{3,2,1,0:T(4,128)(2,1)} %bitcast.27) | data formatting | bytes 589824

commit v5 on v4

--- a/solution.py
+++ b/solution.py
@@ -426,7 +426,7 @@
     ag_start((18, 19))
     take(4)
     hand_on(3)
-    units(192, 192)
+    units(192, 384)
     ag_recv(range(12, 16))
     take(5)
     hand_on(4)
@@ -435,7 +435,6 @@
     for i in (2, 1, 3):
         z_both(6, i).start()
     hand_on(5)
-    units(384, 192)
     units(576, 192)
     units_out(192, 384)
     units_out(576, 192)
@@ -456,10 +455,18 @@
         total = jnp.sum(soft, axis=-1, keepdims=True)
         return (dot_f32(soft.astype(BF16), vals) / total).astype(BF16)
 
-    for o in range(1, RING):
-        OS[o] = attend(o)
+    def send_out(o):
         remote(OS.at[o], OR.at[own_p], o_s.at[o], o_r.at[own_p], tok=tile(o)).start()
-    OR[own_p] = attend(0)
+
+    third, second = attend(3), attend(2)
+    OS[3] = third
+    OS[2] = second
+    send_out(3)
+    send_out(2)
+    first, own = attend(1), attend(0)
+    OS[1] = first
+    send_out(1)
+    OR[own_p] = own
 
     for i in range(1, PROMPTS):
         p, z_query = job(i)
@@ -651,7 +658,7 @@
         out_specs=(vmem, vmem, hbm),
         scratch_shapes=scratch,
         compiler_params=pltpu.CompilerParams(
-            collective_id=0, has_side_effects=True, vmem_limit_bytes=67043328
+            collective_id=0, has_side_effects=True, vmem_limit_bytes=60000000
         ),
     )(*operands)
 

time: 91.7 us -> 92.7 us (1.011)
  Pallas kernels: 86.2 us -> 87.3 us
    pallas_call x1, Pallas kernels: 86.2 us -> 87.3 us  [call_kernel(): pl.pallas_call(kernel, out_shape=(jax.ShapeDtypeStruct((ROWS_OWN // PROMP...]
where the time goes in v5:
time: 92.7 us; the launch traced here: 92.5 us
  Pallas kernels  87.3 us (94%)
  between operations  2.04 us (2%)
  local copies, waits for them, and re-layouts  1.78 us (2%)
  other arithmetic  1.38 us (1%)
    pallas_call x1, Pallas kernels, call_kernel(): pl.pallas_call(kernel, out_shape=(jax.ShapeDtypeStruct((ROWS_OWN // PROMP...  87.3 us

profile of v5, /device:TPU:1, one launch (start us, length us, event | category | flops | bytes accessed | tf_op | source)
XLA Modules:
  0.0 92.5 jit_solution(11989439055563279200)
XLA Ops:
  2.0 0.0 copy-start
  2.0 87.3 %shard_map.175 = (f32[12,4,32]{2,1,0:T(4,128)}, f32[12,4,32]{2,1,0:T(4,128)}, bf16[12,4,3072]{2,1,0:T(4,128)(2,1)}) custom-call(bf16[12,4,3072]{2,1,0:T(4,128)(2,1)} %bitcast.26, f32[4,3072]{1,0:T(4,128)} %bitcast.28, s32[4,1536]{1,0:T(4,128)} %token_hbm.1, s32[1,4]{1,0:T(1,128)} %len_hbm.1, f32[2,128]{1,0:T(2,128)} %bitcast.34, ...), custom_call_target="tpu_custom_call" | custom-call | tf_op jit(solution)/shard_map/pallas_call | solution.py:650
  89.3 0.0 copy-done
  89.3 1.4 %multiply_add_fusion = (f32[6,8,32]{2,1,0:T(8,128)}, f32[6,8,32]{2,1,0:T(8,128)}) fusion(f32[6,8,32]{2,1,0:T(8,128)S(1)} %bitcast.29, f32[]{:T(128)} %bitcast.11, f32[6,8,32]{2,1,0:T(8,128)} %bitcast.33, f32[6,8,32]{2,1,0:T(8,128)} %bitcast.32, f32[]{:T(128)} %bitcast.19), kind=kLoop, calls=%fused_computation | loop fusion | flops 7680 | bytes 30728 | tf_op jit(solution)/shard_map/add | solution.py:714
  90.7 1.8 %copy.22 = bf16[1,12,4,3072]{3,2,1,0:T(4,128)(2,1)} copy(bf16[1,12,4,3072]{3,2,1,0:T(4,128)(2,1)} %bitcast.27) | data formatting | bytes 589824
Async XLA Ops:
  2.0 87.3 %copy-start = (f32[12,4,32]{2,1,0:T(4,128)S(1)}, f32[12,4,32]{2,1,0:T(4,128)}, u32[]{:S(2)}) copy-start(f32[12,4,32]{2,1,0:T(4,128)} %param.17) | copy-start | bytes 18436

commit v6 on v5

--- a/solution.py
+++ b/solution.py
@@ -426,7 +426,7 @@
     ag_start((18, 19))
     take(4)
     hand_on(3)
-    units(192, 384)
+    units(192, 192)
     ag_recv(range(12, 16))
     take(5)
     hand_on(4)
@@ -435,6 +435,7 @@
     for i in (2, 1, 3):
         z_both(6, i).start()
     hand_on(5)
+    units(384, 192)
     units(576, 192)
     units_out(192, 384)
     units_out(576, 192)

time: 92.7 us -> 90.9 us (0.981)
  Pallas kernels: 87.3 us -> 85.5 us
    pallas_call x1, Pallas kernels: 87.3 us -> 85.5 us  [call_kernel(): pl.pallas_call(kernel, out_shape=(jax.ShapeDtypeStruct((ROWS_OWN // PROMP...]
where the time goes in v6:
time: 90.9 us; the launch traced here: 90.7 us
  Pallas kernels  85.5 us (94%)
  between operations  2.04 us (2%)
  local copies, waits for them, and re-layouts  1.78 us (2%)
  other arithmetic  1.38 us (2%)
    pallas_call x1, Pallas kernels, call_kernel(): pl.pallas_call(kernel, out_shape=(jax.ShapeDtypeStruct((ROWS_OWN // PROMP...  85.5 us

profile of v6, /device:TPU:1, one launch (start us, length us, event | category | flops | bytes accessed | tf_op | source)
XLA Modules:
  0.0 90.7 jit_solution(13128271606774891360)
XLA Ops:
  2.0 0.0 copy-start
  2.0 85.5 %shard_map.175 = (f32[12,4,32]{2,1,0:T(4,128)}, f32[12,4,32]{2,1,0:T(4,128)}, bf16[12,4,3072]{2,1,0:T(4,128)(2,1)}) custom-call(bf16[12,4,3072]{2,1,0:T(4,128)(2,1)} %bitcast.26, f32[4,3072]{1,0:T(4,128)} %bitcast.28, s32[4,1536]{1,0:T(4,128)} %token_hbm.1, s32[1,4]{1,0:T(1,128)} %len_hbm.1, f32[2,128]{1,0:T(2,128)} %bitcast.34, ...), custom_call_target="tpu_custom_call" | custom-call | tf_op jit(solution)/shard_map/pallas_call | solution.py:651
  87.5 0.0 copy-done
  87.5 1.4 %multiply_add_fusion = (f32[6,8,32]{2,1,0:T(8,128)}, f32[6,8,32]{2,1,0:T(8,128)}) fusion(f32[6,8,32]{2,1,0:T(8,128)S(1)} %bitcast.29, f32[]{:T(128)} %bitcast.11, f32[6,8,32]{2,1,0:T(8,128)} %bitcast.33, f32[6,8,32]{2,1,0:T(8,128)} %bitcast.32, f32[]{:T(128)} %bitcast.19), kind=kLoop, calls=%fused_computation | loop fusion | flops 7680 | bytes 30728 | tf_op jit(solution)/shard_map/add | solution.py:715
  88.9 1.8 %copy.22 = bf16[1,12,4,3072]{3,2,1,0:T(4,128)(2,1)} copy(bf16[1,12,4,3072]{3,2,1,0:T(4,128)(2,1)} %bitcast.27) | data formatting | bytes 589824
Async XLA Ops:
  2.0 85.5 %copy-start = (f32[12,4,32]{2,1,0:T(4,128)S(1)}, f32[12,4,32]{2,1,0:T(4,128)}, u32[]{:S(2)}) copy-start(f32[12,4,32]{2,1,0:T(4,128)} %param.17) | copy-start | bytes 18436
